TPU v7x, 32 devices: a whole 2x2x4 slice. The times are simulated.
32 devices in a mesh: dom: 4 (over z), elem: 8 (over y, x, core).
Axes of the slice: x: 2, y: 2, z: 4, core: 2. Of those that a mesh axis runs over, the one named last changes fastest.
Arguments:
- positions: float32 [2048, 3, 128], P(('dom', 'elem')), may hold values from -6 to 6
- velocities: float32 [2048, 3, 128], P(('dom', 'elem')), may hold values from -6 to 6
- inv_mass: float32 [2048, 128], P(('dom', 'elem')), may hold values from 0.25 to 2
- send_index: int32 [32, 32, 4], P(('dom', 'elem')), may hold values from 0 to 63
- pair_slave: int32 [32, 128], P(('dom', 'elem')), may hold values from 0 to 63
- pair_live: int32 [32, 128], P(('dom', 'elem')), may hold values from 0 to 1, as said below
- quad_weights: float32 [32, 128, 128], P(('dom', 'elem')), may hold values from 0.25 to 2
- seg_normals: float32 [32, 128, 3, 128], P(('dom', 'elem')), may hold values from -6 to 6
- slave_shape: float32 [128, 128], replicated, may hold values from -0.5 to 0.5
- master_shape: float32 [128, 128], replicated, may hold values from -0.5 to 0.5
- stiffness: float32 [128, 128], replicated, may hold values from -0.5 to 0.5
Outputs:
- velocity_new: float32 [2048, 3, 128], P(('dom', 'elem'))
- contact: float32 [2048, 3, 128], P(('dom', 'elem'))
Inputs may be any that keep to these rules, and one draw needn't show every extreme that they name: `pair_live`: at least one device has all 128 pair slots live; the share of live slots differs from device to device.
All inputs are finite; a program needn't handle non-finite values.
Results may differ from a plain program's by a relative error of at most 0.0003.
Values sent between devices are 32-bit elements; how exact they have to be, the bound alone decides.
No kernel may reach another device: no remote copies, remote signals or barrier semaphores. Data moves between devices by JAX's collectives and lax.ppermute only.
A program may use at most 64 MiB of HBM per device.

v0:
```python
import jax
import jax.numpy as jnp
from jax import lax
from jax.sharding import PartitionSpec as P

HIGH = lax.Precision.HIGHEST


def extended(cells, sides, width):
    for axis, dim in sides:
        count = lax.axis_size(axis)
        ends = count - 1
        head = lax.slice_in_dim(cells, 0, width, axis=dim)
        tail = lax.slice_in_dim(cells, cells.shape[dim] - width, cells.shape[dim], axis=dim)
        cells = jnp.concatenate(
            [
                lax.ppermute(tail, axis, [(i, (i + 1) % count) for i in range(ends)]),
                cells,
                lax.ppermute(head, axis, [((i + 1) % count, i) for i in range(ends)]),
            ],
            axis=dim,
        )
    return cells


def on_device(
    positions,
    velocities,
    inv_mass,
    send_index,
    pair_slave,
    pair_live,
    quad_weights,
    seg_normals,
    slave_shape,
    master_shape,
    stiffness,
):
    patch_count = positions.shape[0]
    nodes = positions.shape[2]
    peer_count = send_index.shape[1]
    slot_count = send_index.shape[2]
    pair_count = peer_count * slot_count
    states = jnp.concatenate([positions, velocities], axis=1)
    outgoing = jnp.take(states, send_index[0].reshape(-1), axis=0).reshape(
        peer_count, slot_count, 6, nodes
    )
    incoming = lax.all_to_all(outgoing, ("dom", "elem"), split_axis=0, concat_axis=0, tiled=True)
    padded = extended(positions, (("elem", 0),), 1)
    neighbour = padded[:-2] + padded[2:] - 2.0 * positions
    internal = (
        -jnp.dot(positions.reshape(-1, nodes), stiffness, precision=HIGH).reshape(
            patch_count, 3, nodes
        )
        + 0.5 * neighbour
    )
    slave_rows = pair_slave[0]
    slave_states = jnp.take(states, slave_rows, axis=0)
    slave_proj = jnp.dot(
        slave_states.reshape(pair_count * 6, nodes), slave_shape, precision=HIGH
    ).reshape(pair_count, 6, -1)
    master_states = incoming.reshape(pair_count * 6, nodes)
    master_proj = jnp.dot(master_states, master_shape, precision=HIGH).reshape(pair_count, 6, -1)
    normals = seg_normals[0]
    gap_vector = slave_proj[:, :3] - master_proj[:, :3]
    gap_rate = slave_proj[:, 3:] - master_proj[:, 3:]
    normal_gap = jnp.sum(normals * gap_vector, axis=1)
    normal_rate = jnp.sum(normals * gap_rate, axis=1)
    pressure = (
        jax.nn.softplus(-(normal_gap + 0.5 * normal_rate))
        * quad_weights[0]
        * pair_live[0].astype(jnp.float32)[:, None]
    )
    traction = (normals * pressure[:, None, :]).reshape(pair_count * 3, -1)
    slave_force = jnp.dot(traction, slave_shape.T, precision=HIGH).reshape(pair_count, 3 * nodes)
    master_force = -jnp.dot(traction, master_shape.T, precision=HIGH).reshape(
        peer_count, slot_count, 3, nodes
    )
    returned = lax.all_to_all(
        master_force, ("dom", "elem"), split_axis=0, concat_axis=0, tiled=True
    )
    patch_ids = jnp.arange(patch_count, dtype=jnp.int32)[:, None]
    slave_table = (slave_rows[None, :] == patch_ids).astype(jnp.float32)
    master_table = (send_index[0].reshape(-1)[None, :] == patch_ids).astype(jnp.float32)
    contact = jnp.dot(slave_table, slave_force, precision=HIGH)
    contact = contact + jnp.dot(
        master_table, returned.reshape(pair_count, 3 * nodes), precision=HIGH
    )
    contact = contact.reshape(patch_count, 3, nodes)
    velocity_new = velocities + 0.5 * inv_mass[:, None, :] * (internal + contact)
    return (velocity_new, contact)


def solution(mesh):
    placed = (
        P(("dom", "elem"), None, None),
        P(("dom", "elem"), None, None),
        P(("dom", "elem"), None),
        P(("dom", "elem"), None, None),
        P(("dom", "elem"), None),
        P(("dom", "elem"), None),
        P(("dom", "elem"), None, None),
        P(("dom", "elem"), None, None, None),
        P(),
        P(),
        P(),
    )
    return jax.shard_map(
        on_device,
        mesh=mesh,
        in_specs=placed,
        out_specs=(P(("dom", "elem"), None, None), P(("dom", "elem"), None, None)),
        check_vma=False,
    )
```

profile of v0, /device:TPU:0, one launch (start us, length us, event | category | flops | bytes accessed | tf_op | source)
XLA Modules:
  0.0 41.6 jit_solution(9498391895209516531)
XLA Ops:
  0.6 0.8 %copy.43 = s32[1,32,4]{2,1,0:T(8,128)S(1)} copy(s32[1,32,4]{1,2,0:T(4,128)} %param.16) | data formatting | bytes 1024 | tf_op args[3]
  1.4 0.1 reshape_squeeze.3
  1.6 1.0 %copy.40 = f32[64,3,128]{2,1,0:T(4,128)S(1)} copy(f32[64,3,128]{2,0,1:T(8,128)} %param.13) | data formatting | bytes 196608 | tf_op args[0]
  2.7 0.8 %gather_fusion.1 = f32[128,6,128]{2,1,0:T(8,128)S(1)} fusion(f32[64,6,128]{2,1,0:T(8,128)S(1)} %pad_maximum_fusion, s32[1024]{0:T(1024)S(1)} %pad_clamp_fusion), kind=kCustom, calls=%fused_computation.1.clone | custom fusion | bytes 786944 | tf_op jit(solution)/shard_map/jit(_take)/gather | solution.py:45
  3.5 0.2 broadcast_select_fusion
  3.7 0.8 %copy.44 = f32[32,4,6,128]{3,1,2,0:T(4,128)} copy(f32[32,4,6,128]{3,2,1,0:T(8,128)S(1)} %bitcast.46) | data formatting | bytes 786432 | tf_op jit(solution)/shard_map/reshape | solution.py:45
  4.6 7.3 %all-to-all-start = ((f32[32,4,6,128]{3,1,2,0:T(4,128)}), f32[32,4,6,128]{3,1,2,0:T(4,128)S(1)}, u32[]{:S(2)}, u32[]{:S(2)}) async-start(f32[32,4,6,128]{3,1,2,0:T(4,128)} %copy.44), calls=%async_computation | async-start | bytes 786432 | tf_op jit(solution)/shard_map/all_to_all | solution.py:48
  11.9 2.2 %collective-permute-start = (f32[1,3,128]{2,0,1:T(1,128)S(1)}, f32[1,3,128]{2,0,1:T(1,128)S(1)}, u32[]{:S(2)}, u32[]{:S(2)}) collective-permute-start(f32[1,3,128]{2,0,1:T(1,128)S(1)} %get-tuple-element.13), channel_id=1, source_target_pairs={{0,1},{1,2},{2,3},{3,4},{4,5},{5,6},{6,7},{8,9},{9,10},{10,11},{11... | collective-permute-start | bytes 4616 | tf_op jit(solution)/shard_map/ppermute | solution.py:17
  14.1 1.3 %collective-permute-start.1 = (f32[1,3,128]{2,0,1:T(1,128)S(1)}, f32[1,3,128]{2,0,1:T(1,128)S(1)}, u32[]{:S(2)}, u32[]{:S(2)}) collective-permute-start(f32[1,3,128]{2,0,1:T(1,128)S(1)} %get-tuple-element.14), channel_id=1, source_target_pairs={{1,0},{2,1},{3,2},{4,3},{5,4},{6,5},{7,6},{9,8},{10,9},{11,10},{12... | collective-permute-start | bytes 4616 | tf_op jit(solution)/shard_map/ppermute | solution.py:19
  15.5 0.6 %copy-done.10 = s32[1,128]{1,0:T(1,128)S(1)} copy-done((s32[1,128]{1,0:T(1,128)S(1)}, s32[1,128]{1,0:T(1,128)}, u32[]{:S(2)}) %copy-start.10) | copy-done | bytes 536
  16.1 0.8 %gather_fusion = f32[128,6,128]{2,1,0:T(8,128)S(1)} fusion(f32[64,6,128]{2,1,0:T(8,128)S(1)} %pad_maximum_fusion, s32[1024]{0:T(1024)S(1)} %pad_clamp_fusion.1), kind=kCustom, calls=%fused_computation.clone | custom fusion | bytes 786944 | tf_op jit(solution)/shard_map/jit(_take)/gather | solution.py:58
  16.9 0.2 copy-done.1
  17.1 0.1 copy.39
  17.2 0.1 squeeze.14
  17.3 0.1 convert_element_type.18
  17.4 0.5 %copy-done.8 = f32[64,128]{1,0:T(8,128)S(1)} copy-done((f32[64,128]{1,0:T(8,128)S(1)}, f32[64,128]{1,0:T(8,128)}, u32[]{:S(2)}) %copy-start.8) | copy-done | bytes 32792
  18.0 0.2 broadcast_select_fusion.1
  18.2 0.6 %copy-done.6 = f32[128,128]{1,0:T(8,128)S(1)} copy-done((f32[128,128]{1,0:T(8,128)S(1)}, f32[128,128]{1,0:T(8,128)}, u32[]{:S(2)}) %copy-start.6) | copy-done | bytes 65560
  18.8 0.5 %fusion.1 = f32[128,6,128]{2,0,1:T(8,128)S(1)} fusion(f32[128,6,128]{2,1,0:T(8,128)S(1)} %broadcast_select_fusion.1, f32[128,128]{1,0:T(8,128)S(1)} %copy-done.6), kind=kOutput, calls=%fused_computation.6 | convolution fusion | flops 150994944 | bytes 851968 | tf_op jit(solution)/shard_map/dot_general | solution.py:59
  19.3 5.9 %all-to-all-done = f32[32,4,6,128]{3,1,2,0:T(4,128)S(1)} async-done(((f32[32,4,6,128]{3,1,2,0:T(4,128)}), f32[32,4,6,128]{3,1,2,0:T(4,128)S(1)}, u32[]{:S(2)}, u32[]{:S(2)}) %all-to-all-start) | async-done | bytes 393248 | tf_op jit(solution)/shard_map/all_to_all | solution.py:48
  25.2 0.5 %fusion.24 = f32[128,6,128]{2,0,1:T(8,128)S(1)} fusion(f32[128,6,128]{2,0,1:T(8,128)S(1)} %bitcast.48, f32[128,128]{1,0:T(8,128)S(1)} %copy-done), kind=kOutput, calls=%fused_computation.40 | convolution fusion | flops 150994944 | bytes 851968 | tf_op jit(solution)/shard_map/dot_general | solution.py:63
  25.8 0.8 %copy-done.5 = f32[1,128,128]{2,1,0:T(8,128)S(1)} copy-done((f32[1,128,128]{2,1,0:T(8,128)S(1)}, f32[1,128,128]{2,1,0:T(8,128)}, u32[]{:S(2)}) %copy-start.5) | copy-done | bytes 65560
  26.8 0.1 fusion.22
  26.9 0.3 convolution_negate_fusion
  27.2 0.8 %copy.48 = f32[32,4,3,128]{3,1,2,0:T(4,128)} copy(f32[32,4,3,128]{3,0,2,1:T(8,128)S(1)} %convolution_negate_fusion) | data formatting | bytes 393216 | tf_op jit(solution)/shard_map/neg | solution.py:76
  28.0 2.6 %all-to-all-start.1 = ((f32[32,4,3,128]{3,1,2,0:T(4,128)}), f32[32,4,3,128]{3,1,2,0:T(4,128)S(1)}, u32[]{:S(2)}, u32[]{:S(2)}) async-start(f32[32,4,3,128]{3,1,2,0:T(4,128)} %copy.48), calls=%async_computation.1 | async-start | bytes 393216 | tf_op jit(solution)/shard_map/all_to_all | solution.py:79
  30.6 0.3 fusion.9
  31.0 0.2 fusion.30
  31.2 8.3 %all-to-all-done.1 = f32[32,4,3,128]{3,1,2,0:T(4,128)S(1)} async-done(((f32[32,4,3,128]{3,1,2,0:T(4,128)}), f32[32,4,3,128]{3,1,2,0:T(4,128)S(1)}, u32[]{:S(2)}, u32[]{:S(2)}) %all-to-all-start.1) | async-done | bytes 196640 | tf_op jit(solution)/shard_map/all_to_all | solution.py:79
  39.7 0.2 fusion
  39.9 0.8 %copy-done.7 = f32[128,128]{1,0:T(8,128)S(1)} copy-done((f32[128,128]{1,0:T(8,128)S(1)}, f32[128,128]{1,0:T(8,128)}, u32[]{:S(2)}) %copy-start.7) | copy-done | bytes 65560
  40.7 0.9 %fusion.17 = f32[64,3,128]{2,0,1:T(8,128)} fusion(f32[64,3,128]{2,0,1:T(8,128)S(1)} %copy-done.3, f32[64,3,128]{2,0,1:T(8,128)S(1)} %bitcast.50, f32[1,3,128]{2,0,1:T(1,128)S(1)} %collective-permute-done.1, f32[64,3,128]{2,0,1:T(8,128)S(1)} %copy-done.2, f32[1,3,128]{2,0,1:T(1,128)S(1)} %collective-permute-done, f32[128,128]{1,0:T(8,128)S(1)} %copy-done.7, ...), kind=kOutput, calls=%fused_computation.32 | convolution fusion | flops 38019072 | bytes 494592 | tf_op jit(solution)/shard_map/dot_general | solution.py:52
  (39 shorter events, 0.7 us)
Async XLA Ops:
  0.6 24.6 %copy-start = (f32[128,128]{1,0:T(8,128)S(1)}, f32[128,128]{1,0:T(8,128)}, u32[]{:S(2)}) copy-start(f32[128,128]{1,0:T(8,128)} %param.22) | copy-start | bytes 196612
  1.6 1.0 %copy-start.3 = (f32[64,3,128]{2,0,1:T(8,128)S(1)}, f32[64,3,128]{2,0,1:T(8,128)}, u32[]{:S(2)}) copy-start(f32[64,3,128]{2,0,1:T(8,128)} %param.14) | copy-start | bytes 294916
  4.6 7.3 %copy-start.2 = (f32[64,3,128]{2,0,1:T(8,128)S(1)}, f32[64,3,128]{2,0,1:T(8,128)}, u32[]{:S(2)}) copy-start(f32[64,3,128]{2,0,1:T(8,128)} %param.13) | copy-start | bytes 294916
  4.6 20.6 %all-to-all-start = ((f32[32,4,6,128]{3,1,2,0:T(4,128)}), f32[32,4,6,128]{3,1,2,0:T(4,128)S(1)}, u32[]{:S(2)}, u32[]{:S(2)}) async-start(f32[32,4,6,128]{3,1,2,0:T(4,128)} %copy.44), calls=%async_computation | async-start | bytes 786432 | tf_op jit(solution)/shard_map/all_to_all | solution.py:48
  11.9 3.5 %copy-start.9 = (s32[1,128]{1,0:T(1,128)S(1)}, s32[1,128]{1,0:T(1,128)}, u32[]{:S(2)}) copy-start(s32[1,128]{1,0:T(1,128)} %param.17) | copy-start | bytes 1540
  11.9 28.0 %collective-permute-start = (f32[1,3,128]{2,0,1:T(1,128)S(1)}, f32[1,3,128]{2,0,1:T(1,128)S(1)}, u32[]{:S(2)}, u32[]{:S(2)}) collective-permute-start(f32[1,3,128]{2,0,1:T(1,128)S(1)} %get-tuple-element.13), channel_id=1, source_target_pairs={{0,1},{1,2},{2,3},{3,4},{4,5},{5,6},{6,7},{8,9},{9,10},{10,11},{11... | collective-permute-start | bytes 4616 | tf_op jit(solution)/shard_map/ppermute | solution.py:17
  14.1 25.8 %collective-permute-start.1 = (f32[1,3,128]{2,0,1:T(1,128)S(1)}, f32[1,3,128]{2,0,1:T(1,128)S(1)}, u32[]{:S(2)}, u32[]{:S(2)}) collective-permute-start(f32[1,3,128]{2,0,1:T(1,128)S(1)} %get-tuple-element.14), channel_id=1, source_target_pairs={{1,0},{2,1},{3,2},{4,3},{5,4},{6,5},{7,6},{9,8},{10,9},{11,10},{12... | collective-permute-start | bytes 4616 | tf_op jit(solution)/shard_map/ppermute | solution.py:19
  15.4 0.7 %copy-start.10 = (s32[1,128]{1,0:T(1,128)S(1)}, s32[1,128]{1,0:T(1,128)}, u32[]{:S(2)}) copy-start(s32[1,128]{1,0:T(1,128)} %param.18) | copy-start | bytes 1540
  16.1 0.9 %copy-start.1 = (f32[1,128,3,128]{3,1,2,0:T(8,128)S(1)}, f32[1,128,3,128]{3,1,2,0:T(8,128)}, u32[]{:S(2)}) copy-start(f32[1,128,3,128]{3,1,2,0:T(8,128)} %param.20) | copy-start | bytes 589828
  17.2 0.8 %copy-start.8 = (f32[64,128]{1,0:T(8,128)S(1)}, f32[64,128]{1,0:T(8,128)}, u32[]{:S(2)}) copy-start(f32[64,128]{1,0:T(8,128)} %param.15) | copy-start | bytes 98308
  18.0 0.8 %copy-start.6 = (f32[128,128]{1,0:T(8,128)S(1)}, f32[128,128]{1,0:T(8,128)}, u32[]{:S(2)}) copy-start(f32[128,128]{1,0:T(8,128)} %param.21) | copy-start | bytes 196612
  25.7 0.8 %copy-start.5 = (f32[1,128,128]{2,1,0:T(8,128)S(1)}, f32[1,128,128]{2,1,0:T(8,128)}, u32[]{:S(2)}) copy-start(f32[1,128,128]{2,1,0:T(8,128)} %param.19) | copy-start | bytes 196612
  28.0 11.5 %all-to-all-start.1 = ((f32[32,4,3,128]{3,1,2,0:T(4,128)}), f32[32,4,3,128]{3,1,2,0:T(4,128)S(1)}, u32[]{:S(2)}, u32[]{:S(2)}) async-start(f32[32,4,3,128]{3,1,2,0:T(4,128)} %copy.48), calls=%async_computation.1 | async-start | bytes 393216 | tf_op jit(solution)/shard_map/all_to_all | solution.py:79
  39.9 0.8 %copy-start.7 = (f32[128,128]{1,0:T(8,128)S(1)}, f32[128,128]{1,0:T(8,128)}, u32[]{:S(2)}) copy-start(f32[128,128]{1,0:T(8,128)} %param.23) | copy-start | bytes 196612
  39.9 1.7 %copy-start.4 = (f32[8,3,8,128]{3,2,0,1:T(8,128)}, f32[8,3,8,128]{3,2,0,1:T(8,128)S(1)}, u32[]{:S(2)}) copy-start(f32[8,3,8,128]{3,2,0,1:T(8,128)S(1)} %copy.64) | copy-start | bytes 294916
where the time goes:
time: 42.2 us; the launch traced here: 41.6 us
  waiting for transfers between devices  14.2 us (34%)
  starting transfers between devices  13.4 us (32%)
  local copies, waits for them, and re-layouts  9.37 us (22%)
  matrix products  2.89 us (7%)
  between operations  1.01 us (2%)
  other arithmetic  0.76 us (2%)
    all_to_all x1, waiting for transfers between devices, on_device(): lax.all_to_all(master_force, ('dom', 'elem'), split_axis=0, concat_axis=0...  8.33 us
    all_to_all x1, starting transfers between devices, on_device(): lax.all_to_all(outgoing, ('dom', 'elem'), split_axis=0, concat_axis=0, ti...  7.33 us
    all_to_all x1, waiting for transfers between devices, on_device(): lax.all_to_all(outgoing, ('dom', 'elem'), split_axis=0, concat_axis=0, ti...  5.89 us
    unnamed x26, local copies, waits for them, and re-layouts  5.57 us
    all_to_all x1, starting transfers between devices, on_device(): lax.all_to_all(master_force, ('dom', 'elem'), split_axis=0, concat_axis=0...  2.58 us
    ppermute x1, starting transfers between devices, extended(): lax.ppermute(tail, axis, [(i, (i + 1) % count) for i in range(ends)])  2.16 us
    ppermute x1, starting transfers between devices, extended(): lax.ppermute(head, axis, [((i + 1) % count, i) for i in range(ends)])  1.29 us
    dot_general x1, matrix products, on_device(): jnp.dot(positions.reshape(-1, nodes), stiffness, precision=HIGH)  0.88 us
  transfers between devices with their start and end apart: 4, of which 2 were waited for; matrix products, arithmetic and copies ran while one was open for 11% of the time, Pallas kernels for 0%

commit v1 on v0

v1 whole, which is shorter than its diff:
```python
import functools

import jax
import jax.numpy as jnp
from jax import lax
from jax.experimental import pallas as pl
from jax.experimental.pallas import tpu as pltpu
from jax.sharding import PartitionSpec as P

VMEM = pl.BlockSpec(memory_space=pltpu.VMEM)
NN = (((1,), (0,)), ((), ()))
NT = (((1,), (1,)), ((), ()))
TN = (((0,), (0,)), ((), ()))


def split(x):
    high = x.astype(jnp.bfloat16)
    return high, (x - high.astype(jnp.float32)).astype(jnp.bfloat16)


def dot3(a, b, dims):
    a_high, a_low = split(a)
    b_high, b_low = split(b)
    dot = functools.partial(lax.dot_general, dimension_numbers=dims, preferred_element_type=jnp.float32)
    return dot(a_high, b_high) + (dot(a_high, b_low) + dot(a_low, b_high))


def pick(table, b, dims):
    high, low = split(b)
    dot = functools.partial(lax.dot_general, dimension_numbers=dims, preferred_element_type=jnp.float32)
    return dot(table, high) + dot(table, low)


def index_row(send_ref, slave_ref, patches):
    slots, peers = send_ref.shape
    width = 2 * slots
    columns = peers * width
    column = lax.broadcasted_iota(jnp.int32, (peers, columns), 1)
    peer = lax.broadcasted_iota(jnp.int32, (peers, columns), 0)
    spread = (column // width == peer).astype(jnp.bfloat16)
    masters = jnp.dot(send_ref[...].astype(jnp.bfloat16), spread, preferred_element_type=jnp.float32)
    slot = lax.broadcasted_iota(jnp.int32, (slots, columns), 0)
    place = lax.broadcasted_iota(jnp.int32, (slots, columns), 1) % width
    masters = jnp.sum(jnp.where(place == slot, masters, 0.0), axis=0, keepdims=True)
    pairs = peers * slots
    column = lax.broadcasted_iota(jnp.int32, (pairs, columns), 1)
    pair = lax.broadcasted_iota(jnp.int32, (pairs, columns), 0)
    spread = (column // width * slots + column % width - slots == pair) & (column % width >= slots)
    slaves = (slave_ref[...] + patches).astype(jnp.bfloat16)
    slaves = jnp.dot(slaves, spread.astype(jnp.bfloat16), preferred_element_type=jnp.float32)
    return (masters + slaves).astype(jnp.int32)


def table_of(row, patches):
    return (lax.broadcasted_iota(jnp.int32, (2 * patches, row.shape[1]), 0) == row).astype(jnp.bfloat16)


def pack_kernel(position_ref, velocity_ref, send_ref, slave_ref, live_ref, weight_ref, normal_ref, slave_shape_ref, master_shape_ref, out_ref):
    _, patches, nodes = position_ref.shape
    slots, peers = send_ref.shape
    segments = weight_ref.shape[-1]
    state = (position_ref[...] + 0.5 * velocity_ref[...]).reshape(3 * patches, nodes)
    master = dot3(state, master_shape_ref[...], NN).reshape(3, patches, segments)
    slave = dot3(state, slave_shape_ref[...], NN).reshape(3, patches, segments)
    table = table_of(index_row(send_ref, slave_ref, patches), patches)
    width = 2 * slots
    first = lax.broadcasted_iota(jnp.int32, (peers, width, segments), 1) < slots
    gap = jnp.zeros((peers, width, segments), jnp.float32)
    for c in range(3):
        both = jnp.concatenate([master[c], slave[c]], axis=0)
        picked = pick(table, both, TN).reshape(peers, width, segments)
        normal = normal_ref[c].reshape(peers, slots, segments)
        normal = jnp.concatenate([normal, normal], axis=1)
        gap = gap + normal * picked
        out_ref[:, c * width : (c + 1) * width, :] = jnp.where(first, picked, normal)
    live = live_ref[...].astype(jnp.float32).reshape(segments_of(live_ref), 1)
    weight = (weight_ref[...] * live).reshape(peers, slots, segments)
    weight = jnp.concatenate([weight, weight], axis=1)
    out_ref[:, 3 * width : 4 * width, :] = jnp.where(first, weight, gap)


def segments_of(ref):
    return ref.shape[1]


def chain_kernel(position_ref, velocity_ref, before_ref, after_ref, mass_ref, stiffness_ref, out_ref):
    _, patches, nodes = position_ref.shape
    position = position_ref[...]
    row = lax.broadcasted_iota(jnp.int32, (patches, nodes), 0)
    product = dot3(position.reshape(3 * patches, nodes), stiffness_ref[...], NN).reshape(3, patches, nodes)
    half = 0.5 * mass_ref[...]
    for c in range(3):
        x = position[c]
        before = jnp.where(row == 0, before_ref[c], pltpu.roll(x, 1, 0))
        after = jnp.where(row == patches - 1, after_ref[c], pltpu.roll(x, patches - 1, 0))
        internal = 0.5 * (before + after - 2.0 * x) - product[c]
        out_ref[c] = velocity_ref[c] + half * internal


def force_kernel(sent_ref, got_ref, send_ref, slave_ref, base_ref, mass_ref, slave_shape_ref, master_shape_ref, velocity_ref, contact_ref):
    _, patches, nodes = base_ref.shape
    slots, peers = send_ref.shape
    segments = sent_ref.shape[-1]
    width = 2 * slots
    first = lax.broadcasted_iota(jnp.int32, (peers, width, segments), 1) < slots
    table = table_of(index_row(send_ref, slave_ref, patches), patches)

    def swapped(x):
        return jnp.concatenate([x[:, slots:], x[:, :slots]], axis=1)

    normals = []
    gap = jnp.zeros((peers, width, segments), jnp.float32)
    for c in range(3):
        sent = sent_ref[:, c * width : (c + 1) * width, :]
        got = swapped(got_ref[:, c * width : (c + 1) * width, :])
        gap = gap - sent * got
        normals.append(jnp.where(first, got, sent))
    sent = sent_ref[:, 3 * width : 4 * width, :]
    got = got_ref[:, 3 * width : 4 * width, :]
    gap = gap + jnp.where(first, swapped(got), sent)
    weight = jnp.where(first, got, swapped(sent))
    pressure = (jnp.maximum(-gap, 0.0) + jnp.log1p(jnp.exp(-jnp.abs(gap)))) * weight
    half = 0.5 * mass_ref[...]
    for c in range(3):
        traction = (normals[c] * pressure).reshape(peers * width, segments)
        summed = pick(table, traction, NN)
        contact = dot3(summed[patches:], slave_shape_ref[...], NT) - dot3(summed[:patches], master_shape_ref[...], NT)
        contact_ref[c] = contact
        velocity_ref[c] = base_ref[c] + half * contact


def on_device(
    positions,
    velocities,
    inv_mass,
    send_index,
    pair_slave,
    pair_live,
    quad_weights,
    seg_normals,
    slave_shape,
    master_shape,
    stiffness,
):
    patches, _, nodes = positions.shape
    _, peers, slots = send_index.shape
    segments = quad_weights.shape[-1]
    place = jnp.transpose(positions, (1, 0, 2))
    speed = jnp.transpose(velocities, (1, 0, 2))
    send = jnp.transpose(send_index[0], (1, 0))
    normals = jnp.transpose(seg_normals[0], (1, 0, 2))
    sent = pl.pallas_call(
        pack_kernel,
        out_shape=jax.ShapeDtypeStruct((peers, 8 * slots, segments), jnp.float32),
        in_specs=[VMEM] * 9,
        out_specs=VMEM,
    )(place, speed, send, pair_slave, pair_live, quad_weights[0], normals, slave_shape, master_shape)
    got = lax.all_to_all(sent, ("dom", "elem"), split_axis=0, concat_axis=0, tiled=True)
    count = lax.axis_size("elem")
    before = lax.ppermute(place[:, -1:], "elem", [(i, i + 1) for i in range(count - 1)])
    after = lax.ppermute(place[:, :1], "elem", [(i + 1, i) for i in range(count - 1)])
    base = pl.pallas_call(
        chain_kernel,
        out_shape=jax.ShapeDtypeStruct((3, patches, nodes), jnp.float32),
        in_specs=[VMEM] * 6,
        out_specs=VMEM,
        cost_estimate=pl.CostEstimate(flops=6 * 3 * patches * nodes * nodes, bytes_accessed=16 * 3 * patches * nodes, transcendentals=0),
    )(place, speed, before, after, inv_mass, stiffness)
    velocity, contact = pl.pallas_call(
        force_kernel,
        out_shape=[jax.ShapeDtypeStruct((3, patches, nodes), jnp.float32)] * 2,
        in_specs=[VMEM] * 8,
        out_specs=[VMEM] * 2,
    )(sent, got, send, pair_slave, base, inv_mass, slave_shape, master_shape)
    return jnp.transpose(velocity, (1, 0, 2)), jnp.transpose(contact, (1, 0, 2))


def solution(mesh):
    both = ("dom", "elem")
    placed = (
        P(both, None, None),
        P(both, None, None),
        P(both, None),
        P(both, None, None),
        P(both, None),
        P(both, None),
        P(both, None, None),
        P(both, None, None, None),
        P(),
        P(),
        P(),
    )
    return jax.shard_map(
        on_device,
        mesh=mesh,
        in_specs=placed,
        out_specs=(P(both, None, None), P(both, None, None)),
        check_vma=False,
    )
```

time: 42.2 us -> 30.2 us (0.72)
  local copies, waits for them, and re-layouts: 9.37 us -> 2.1 us
  Pallas kernels: 0 us -> 7.25 us
  waiting for transfers between devices: 14.2 us -> 8.16 us
  matrix products: 2.89 us -> 0 us
  starting transfers between devices: 13.4 us -> 11.6 us
  other arithmetic: 0.76 us -> 0 us
    pallas_call x0 -> x3, Pallas kernels: none -> 7.25 us  [the longest x1 2.94 us: on_device(): pl.pallas_call(force_kernel, out_shape=[jax.ShapeDtypeStruct((3, patches,...]
    all_to_all x2 -> x1, waiting for transfers between devices: 14.2 us -> 7.37 us  [on_device(): lax.all_to_all(sent, ('dom', 'elem'), split_axis=0, concat_axis=0, tiled=...]
    unnamed x26 -> x6, local copies, waits for them, and re-layouts: 5.57 us -> 1.37 us
    dot_general x7 -> x0, matrix products: 2.89 us -> none  [the longest x1 0.88 us: on_device(): jnp.dot(positions.reshape(-1, nodes), stiffness, precision=HIGH)]
    all_to_all x2 -> x1, starting transfers between devices: 9.9 us -> 7.33 us  [on_device(): lax.all_to_all(sent, ('dom', 'elem'), split_axis=0, concat_axis=0, tiled=...]
    gather x2 -> x0, local copies, waits for them, and re-layouts: 1.52 us -> none  [the longest x1 0.76 us: on_device(): jnp.take(states, send_index[0].reshape(-1), axis=0)]
    reshape x3 -> x0, local copies, waits for them, and re-layouts: 0.9 us -> none  [the longest x1 0.85 us: on_device(): jnp.take(states, send_index[0].reshape(-1), axis=0)]
    ppermute x2, starting transfers between devices: 3.45 us -> 4.31 us  [the longest x1 3.03 us: on_device(): lax.ppermute(place[:, -1:], 'elem', [(i, i + 1) for i in range(count - 1)])]
  transfers between devices with their start and end apart: 4 -> 3, of which waited for: 2 -> 2; matrix products, arithmetic and copies ran while one was open for 11% -> 2% of each run, Pallas kernels for 0% -> 6%
where the time goes in v1:
time: 30.2 us; the launch traced here: 29.8 us
  starting transfers between devices  11.6 us (38%)
  waiting for transfers between devices  8.16 us (27%)
  Pallas kernels  7.25 us (24%)
  local copies, waits for them, and re-layouts  2.1 us (7%)
  between operations  0.68 us (2%)
    all_to_all x1, waiting for transfers between devices, on_device(): lax.all_to_all(sent, ('dom', 'elem'), split_axis=0, concat_axis=0, tiled=...  7.37 us
    all_to_all x1, starting transfers between devices, on_device(): lax.all_to_all(sent, ('dom', 'elem'), split_axis=0, concat_axis=0, tiled=...  7.33 us
    ppermute x1, starting transfers between devices, on_device(): lax.ppermute(place[:, -1:], 'elem', [(i, i + 1) for i in range(count - 1)])  3.03 us
    pallas_call x1, Pallas kernels, on_device(): pl.pallas_call(force_kernel, out_shape=[jax.ShapeDtypeStruct((3, patches,...  2.94 us
    pallas_call x1, Pallas kernels, on_device(): pl.pallas_call(pack_kernel, out_shape=jax.ShapeDtypeStruct((peers, 8 * sl...  2.5 us
    pallas_call x1, Pallas kernels, on_device(): pl.pallas_call(chain_kernel, out_shape=jax.ShapeDtypeStruct((3, patches,...  1.81 us
    unnamed x6, local copies, waits for them, and re-layouts  1.37 us
    ppermute x1, starting transfers between devices, on_device(): lax.ppermute(place[:, :1], 'elem', [(i + 1, i) for i in range(count - 1)])  1.28 us
  transfers between devices with their start and end apart: 3, of which 2 were waited for; matrix products, arithmetic and copies ran while one was open for 2% of the time, Pallas kernels for 6%

profile of v1, /device:TPU:0, one launch (start us, length us, event | category | flops | bytes accessed | tf_op | source)
XLA Modules:
  0.0 29.8 jit_solution(3852318301052450660)
XLA Ops:
  0.6 2.5 %shard_map.122.sent_ref = f32[32,32,128]{2,1,0:T(8,128)} custom-call(f32[3,64,128]{2,1,0:T(8,128)} %bitcast.11, f32[3,64,128]{2,1,0:T(8,128)} %bitcast.14, s32[4,32]{1,0:T(4,128)} %bitcast.18, s32[1,128]{1,0:T(1,128)} %slave_ref.3, s32[1,128]{1,0:T(1,128)} %live_ref.1, f32[128,128]{1,0:T(8,128)} %bitcast.17, f32[3,128,128]{2,1,0:T(8,128)} %bitcast.16, ...), custom_call_target="tpu_custom_call" | custom-call | tf_op jit(solution)/shard_map/pallas_call | solution.py:152
  3.1 7.3 %all-to-all-start = ((f32[32,32,128]{2,1,0:T(8,128)}), f32[32,32,128]{2,1,0:T(8,128)S(1)}, u32[]{:S(2)}, u32[]{:S(2)}) async-start(f32[32,32,128]{2,1,0:T(8,128)} %shard_map.122.sent_ref), calls=%async_computation | async-start | bytes 1048576 | tf_op jit(solution)/shard_map/all_to_all | solution.py:158
  10.5 0.7 %fusion = (f32[3,1,128]{2,1,0:T(1,128)S(1)}, f32[3,1,128]{2,1,0:T(1,128)S(1)}) fusion(f32[3,64,128]{2,1,0:T(8,128)} %bitcast.12), kind=kLoop, calls=%fused_computation | loop fusion | bytes 6144 | tf_op jit(solution)/shard_map/slice | solution.py:161
  11.2 1.3 %collective-permute-start.1 = (f32[3,1,128]{2,1,0:T(1,128)S(1)}, f32[3,1,128]{2,1,0:T(1,128)S(1)}, u32[]{:S(2)}, u32[]{:S(2)}) collective-permute-start(f32[3,1,128]{2,1,0:T(1,128)S(1)} %get-tuple-element.6), channel_id=1, source_target_pairs={{1,0},{2,1},{3,2},{4,3},{5,4},{6,5},{7,6},{9,8},{10,9},{11,10},{12... | collective-permute-start | bytes 4616 | tf_op jit(solution)/shard_map/ppermute | solution.py:161
  12.5 3.0 %collective-permute-start = (f32[3,1,128]{2,1,0:T(1,128)S(1)}, f32[3,1,128]{2,1,0:T(1,128)S(1)}, u32[]{:S(2)}, u32[]{:S(2)}) collective-permute-start(f32[3,1,128]{2,1,0:T(1,128)S(1)} %get-tuple-element.7), channel_id=1, source_target_pairs={{0,1},{1,2},{2,3},{3,4},{4,5},{5,6},{6,7},{8,9},{9,10},{10,11},{11... | collective-permute-start | bytes 4616 | tf_op jit(solution)/shard_map/ppermute | solution.py:160
  15.5 0.0 collective-permute-done.1.after_ref
  15.5 0.0 copy-start.1
  15.5 0.8 %collective-permute-done.before_ref = f32[3,1,128]{2,1,0:T(1,128)S(1)} collective-permute-done((f32[3,1,128]{2,1,0:T(1,128)S(1)}, f32[3,1,128]{2,1,0:T(1,128)S(1)}, u32[]{:S(2)}, u32[]{:S(2)}) %collective-permute-start) | collective-permute-done | bytes 1568 | tf_op jit(solution)/shard_map/ppermute | solution.py:160
  16.3 0.0 copy-done.1
  16.3 0.0 copy-start.2
  16.3 0.6 %copy-done.2 = f32[3,1,128]{2,1,0:T(1,128)} copy-done((f32[3,1,128]{2,1,0:T(1,128)}, f32[3,1,128]{2,1,0:T(1,128)S(1)}, u32[]{:S(2)}) %copy-start.2) | copy-done | bytes 1560
  16.9 1.8 %shard_map.123.base_ref = f32[3,64,128]{2,1,0:T(8,128)} custom-call(f32[3,64,128]{2,1,0:T(8,128)} %bitcast.13, f32[3,64,128]{2,1,0:T(8,128)} %bitcast.15, f32[3,1,128]{2,1,0:T(1,128)} %copy-done.2, f32[3,1,128]{2,1,0:T(1,128)} %copy-done.1, f32[64,128]{1,0:T(8,128)} %mass_ref.3, f32[128,128]{1,0:T(8,128)} %stiffness_ref.1), custom_call_target="tpu_custom_call" | custom-call | flops 18874368 | bytes 393216 | tf_op jit(solution)/shard_map/pallas_call | solution.py:162
  18.7 7.4 %all-to-all-done.got_ref = f32[32,32,128]{2,1,0:T(8,128)S(1)} async-done(((f32[32,32,128]{2,1,0:T(8,128)}), f32[32,32,128]{2,1,0:T(8,128)S(1)}, u32[]{:S(2)}, u32[]{:S(2)}) %all-to-all-start) | async-done | bytes 524320 | tf_op jit(solution)/shard_map/all_to_all | solution.py:158
  26.1 0.0 copy-start
  26.1 0.8 %copy-done = f32[32,32,128]{2,1,0:T(8,128)} copy-done((f32[32,32,128]{2,1,0:T(8,128)}, f32[32,32,128]{2,1,0:T(8,128)S(1)}, u32[]{:S(2)}) %copy-start) | copy-done | bytes 524312
  26.9 2.9 %shard_map.124 = (f32[3,64,128]{2,1,0:T(8,128)}, f32[3,64,128]{2,1,0:T(8,128)}) custom-call(f32[32,32,128]{2,1,0:T(8,128)} %shard_map.122.sent_ref, f32[32,32,128]{2,1,0:T(8,128)} %copy-done, s32[4,32]{1,0:T(4,128)} %bitcast.19, s32[1,128]{1,0:T(1,128)} %slave_ref.3, f32[3,64,128]{2,1,0:T(8,128)} %shard_map.123.base_ref, f32[64,128]{1,0:T(8,128)} %mass_ref.3, ...), custom_call_target="tpu_custom_call" | custom-call | tf_op jit(solution)/shard_map/pallas_call | solution.py:169
Async XLA Ops:
  3.1 23.0 %all-to-all-start = ((f32[32,32,128]{2,1,0:T(8,128)}), f32[32,32,128]{2,1,0:T(8,128)S(1)}, u32[]{:S(2)}, u32[]{:S(2)}) async-start(f32[32,32,128]{2,1,0:T(8,128)} %shard_map.122.sent_ref), calls=%async_computation | async-start | bytes 1048576 | tf_op jit(solution)/shard_map/all_to_all | solution.py:158
  11.2 4.3 %collective-permute-start.1 = (f32[3,1,128]{2,1,0:T(1,128)S(1)}, f32[3,1,128]{2,1,0:T(1,128)S(1)}, u32[]{:S(2)}, u32[]{:S(2)}) collective-permute-start(f32[3,1,128]{2,1,0:T(1,128)S(1)} %get-tuple-element.6), channel_id=1, source_target_pairs={{1,0},{2,1},{3,2},{4,3},{5,4},{6,5},{7,6},{9,8},{10,9},{11,10},{12... | collective-permute-start | bytes 4616 | tf_op jit(solution)/shard_map/ppermute | solution.py:161
  12.5 3.8 %collective-permute-start = (f32[3,1,128]{2,1,0:T(1,128)S(1)}, f32[3,1,128]{2,1,0:T(1,128)S(1)}, u32[]{:S(2)}, u32[]{:S(2)}) collective-permute-start(f32[3,1,128]{2,1,0:T(1,128)S(1)} %get-tuple-element.7), channel_id=1, source_target_pairs={{0,1},{1,2},{2,3},{3,4},{4,5},{5,6},{6,7},{8,9},{9,10},{10,11},{11... | collective-permute-start | bytes 4616 | tf_op jit(solution)/shard_map/ppermute | solution.py:160
  15.5 0.8 %copy-start.1 = (f32[3,1,128]{2,1,0:T(1,128)}, f32[3,1,128]{2,1,0:T(1,128)S(1)}, u32[]{:S(2)}) copy-start(f32[3,1,128]{2,1,0:T(1,128)S(1)} %collective-permute-done.1.after_ref) | copy-start | bytes 4612
  16.3 0.6 %copy-start.2 = (f32[3,1,128]{2,1,0:T(1,128)}, f32[3,1,128]{2,1,0:T(1,128)S(1)}, u32[]{:S(2)}) copy-start(f32[3,1,128]{2,1,0:T(1,128)S(1)} %collective-permute-done.before_ref) | copy-start | bytes 4612
  26.1 0.8 %copy-start = (f32[32,32,128]{2,1,0:T(8,128)}, f32[32,32,128]{2,1,0:T(8,128)S(1)}, u32[]{:S(2)}) copy-start(f32[32,32,128]{2,1,0:T(8,128)S(1)} %all-to-all-done.got_ref) | copy-start | bytes 1572868

commit v2 on v1

v2 whole, which is shorter than its diff:
```python
import functools

import jax
import jax.numpy as jnp
from jax import lax
from jax.experimental import pallas as pl
from jax.experimental.pallas import tpu as pltpu
from jax.sharding import PartitionSpec as P

VMEM = pl.BlockSpec(memory_space=pltpu.VMEM)
HBM = pl.BlockSpec(memory_space=pltpu.HBM)
SMALL = pltpu.CompilerParams(vmem_limit_bytes=16 << 20)
EXCHANGE = ("elem", "dom")
NN = (((1,), (0,)), ((), ()))
NT = (((1,), (1,)), ((), ()))
TN = (((0,), (0,)), ((), ()))


def dot(a, b, dims):
    return lax.dot_general(a, b, dims, preferred_element_type=jnp.float32)


def split(x):
    high = x.astype(jnp.bfloat16)
    return high, (x - high.astype(jnp.float32)).astype(jnp.bfloat16)


def dot3(a, b, dims):
    a_high, a_low = split(a)
    b_high, b_low = split(b)
    return dot(a_high, b_high, dims) + (dot(a_high, b_low, dims) + dot(a_low, b_high, dims))


def exchange_order():
    sizes = {"dom": lax.axis_size("dom"), "elem": lax.axis_size("elem")}
    assert EXCHANGE == ("elem", "dom")
    return [d * sizes["elem"] + e for e in range(sizes["elem"]) for d in range(sizes["dom"])]


def index_table(send, slave, patches, order):
    slots, peers = send.shape
    width = 2 * slots
    columns = peers * width
    outer = lax.axis_size(EXCHANGE[0])
    inner = lax.axis_size(EXCHANGE[1])

    def spot(peer):
        return peer % outer * inner + peer // outer

    column = lax.broadcasted_iota(jnp.int32, (peers, columns), 1)
    peer = lax.broadcasted_iota(jnp.int32, (peers, columns), 0)
    spread = (column // width == spot(peer)).astype(jnp.bfloat16)
    masters = dot(send.astype(jnp.bfloat16), spread, NN)
    slot = lax.broadcasted_iota(jnp.int32, (slots, columns), 0)
    place = lax.broadcasted_iota(jnp.int32, (slots, columns), 1) % width
    masters = jnp.sum(jnp.where(place == slot, masters, 0.0), axis=0, keepdims=True)
    pairs = peers * slots
    column = lax.broadcasted_iota(jnp.int32, (pairs, columns), 1)
    pair = lax.broadcasted_iota(jnp.int32, (pairs, columns), 0)
    spread = column == spot(pair // slots) * width + slots + pair % slots
    slaves = dot((slave + patches).astype(jnp.bfloat16), spread.astype(jnp.bfloat16), NN)
    row = (masters + slaves).astype(jnp.int32)
    return (lax.broadcasted_iota(jnp.int32, (2 * patches, columns), 0) == row).astype(jnp.bfloat16)


def pack_kernel(order, *refs):
    ins, out_hbm, vmem, packed, in_sems, out_sems = refs[:9], refs[9], refs[10:19], refs[19], refs[20], refs[21]
    loads = [pltpu.make_async_copy(ins[i], vmem[i], in_sems.at[i]) for i in range(9)]
    for load in loads:
        load.start()
    send_ref, slave_ref, position_ref, velocity_ref, master_ref, slave_shape_ref, normal_ref, weight_ref, live_ref = vmem
    _, patches, nodes = position_ref.shape
    slots, peers = send_ref.shape
    segments = weight_ref.shape[-1]
    width = 2 * slots
    loads[0].wait()
    loads[1].wait()
    table = index_table(send_ref[...], slave_ref[...], patches, order)
    for i in (2, 3, 4, 5):
        loads[i].wait()
    state = (position_ref[...] + 0.5 * velocity_ref[...]).reshape(3 * patches, nodes)
    shapes = jnp.concatenate([master_ref[...], slave_shape_ref[...]], axis=1)
    projected = dot3(state, shapes, NN).reshape(3, patches, 2 * segments)
    first = lax.broadcasted_iota(jnp.int32, (peers, width, segments), 1) < slots
    gap = jnp.zeros((peers, width, segments), jnp.float32)

    def ordered(x):
        x = x.reshape(peers, slots, segments)
        x = jnp.concatenate([x[p : p + 1] for p in order], axis=0)
        return jnp.concatenate([x, x], axis=1)

    stores = [
        pltpu.make_async_copy(packed.at[:, pl.ds(t * width, width), :], out_hbm.at[:, pl.ds(t * width, width), :], out_sems.at[t])
        for t in range(4)
    ]
    loads[6].wait()
    for c in range(3):
        both = jnp.concatenate([projected[c, :, :segments], projected[c, :, segments:]], axis=0)
        high, low = split(both)
        picked = (dot(table, high, TN) + dot(table, low, TN)).reshape(peers, width, segments)
        normal = ordered(normal_ref[c])
        gap = gap + normal * picked
        packed[:, c * width : (c + 1) * width, :] = jnp.where(first, picked, normal)
        stores[c].start()
    loads[7].wait()
    loads[8].wait()
    live = live_ref[...].astype(jnp.float32).reshape(peers * slots, 1)
    packed[:, 3 * width : 4 * width, :] = jnp.where(first, ordered(weight_ref[...] * live), gap)
    stores[3].start()
    for store in stores:
        store.wait()


def window_kernel(
    order,
    sent_ref, send_ref, slave_ref, position_ref, velocity_ref, before_ref, after_ref, mass_ref, stiffness_ref, slave_shape_ref, master_shape_ref,
    own_ref, table_ref, high_ref, low_ref, base_ref, half_ref,
):
    _, patches, nodes = position_ref.shape
    slots, peers = send_ref.shape
    width = 2 * slots
    own_ref[:, : 4 * width, :] = sent_ref[...]
    last = sent_ref[:, 3 * width : 4 * width, :]
    own_ref[:, 4 * width :, :] = pltpu.roll(last, slots, 1)
    table_ref[...] = index_table(send_ref[...], slave_ref[...], patches, order)
    high, low = split(jnp.concatenate([-master_shape_ref[...], slave_shape_ref[...]], axis=1))
    high_ref[...] = high
    low_ref[...] = low
    row = lax.broadcasted_iota(jnp.int32, (patches, nodes), 0)
    position = position_ref[...]
    product = dot3(position.reshape(3 * patches, nodes), stiffness_ref[...], NN).reshape(3, patches, nodes)
    half = 0.5 * mass_ref[...]
    half_ref[...] = half
    for c in range(3):
        x = position[c]
        before = jnp.where(row == 0, before_ref[c], pltpu.roll(x, 1, 0))
        after = jnp.where(row == patches - 1, after_ref[c], pltpu.roll(x, patches - 1, 0))
        internal = 0.5 * (before + after - 2.0 * x) - product[c]
        base_ref[c] = velocity_ref[c] + half * internal


def force_kernel(got_ref, own_ref, table_ref, shape_high_ref, shape_low_ref, base_ref, half_ref, velocity_ref, contact_ref, high_ref, low_ref):
    _, patches, nodes = base_ref.shape
    peers = got_ref.shape[0]
    segments = got_ref.shape[-1]
    width = got_ref.shape[1] // 4
    slots = width // 2
    group = 8
    first = lax.broadcasted_iota(jnp.int32, (group, width, segments), 1) < slots
    for g in range(0, peers, group):
        def own(t):
            return own_ref[g : g + group, t * width : (t + 1) * width, :]

        def got(t):
            return got_ref[g : g + group, t * width : (t + 1) * width, :]

        gap = jnp.where(first, pltpu.roll(got(3), slots, 1), own(3))
        weight = jnp.where(first, got(3), own(4))
        normals = []
        for c in range(3):
            mine = own(c)
            theirs = pltpu.roll(got(c), slots, 1)
            gap = gap - mine * theirs
            normals.append(jnp.where(first, theirs, mine))
        pressure = (jnp.maximum(-gap, 0.0) + jnp.log1p(jnp.exp(-jnp.abs(gap)))) * weight
        for c in range(3):
            high, low = split((normals[c] * pressure).reshape(group * width, segments))
            high_ref[g * width : (g + group) * width, c * segments : (c + 1) * segments] = high
            low_ref[g * width : (g + group) * width, c * segments : (c + 1) * segments] = low
    table = table_ref[...]
    summed = dot(table, high_ref[...], NN) + dot(table, low_ref[...], NN)
    summed = jnp.concatenate(
        [
            jnp.concatenate([summed[:patches, c * segments : (c + 1) * segments], summed[patches:, c * segments : (c + 1) * segments]], axis=1)
            for c in range(3)
        ],
        axis=0,
    )
    high, low = split(summed)
    contact = dot(high, shape_high_ref[...], NT) + (dot(high, shape_low_ref[...], NT) + dot(low, shape_high_ref[...], NT))
    contact = contact.reshape(3, patches, nodes)
    contact_ref[...] = contact
    velocity_ref[...] = base_ref[...] + half_ref[...] * contact


def on_device(
    positions,
    velocities,
    inv_mass,
    send_index,
    pair_slave,
    pair_live,
    quad_weights,
    seg_normals,
    slave_shape,
    master_shape,
    stiffness,
):
    patches, _, nodes = positions.shape
    _, peers, slots = send_index.shape
    segments = quad_weights.shape[-1]
    rows = 8 * slots
    f32, bf16 = jnp.float32, jnp.bfloat16
    order = exchange_order()
    place = jnp.transpose(positions, (1, 0, 2))
    speed = jnp.transpose(velocities, (1, 0, 2))
    send = jnp.transpose(send_index[0], (1, 0))
    normals = jnp.transpose(seg_normals[0], (1, 0, 2))
    operands = (send, pair_slave, place, speed, master_shape, slave_shape, normals, quad_weights[0], pair_live)
    sent = pl.pallas_call(
        functools.partial(pack_kernel, order),
        out_shape=jax.ShapeDtypeStruct((peers, rows, segments), f32),
        in_specs=[HBM] * 9,
        out_specs=HBM,
        scratch_shapes=[pltpu.VMEM(x.shape, x.dtype) for x in operands]
        + [pltpu.VMEM((peers, rows, segments), f32), pltpu.SemaphoreType.DMA((9,)), pltpu.SemaphoreType.DMA((4,))],
    )(*operands)
    got = lax.all_to_all(sent, EXCHANGE, split_axis=0, concat_axis=0, tiled=True)
    count = lax.axis_size("elem")
    before = lax.ppermute(place[:, -1:], "elem", [(i, i + 1) for i in range(count - 1)])
    after = lax.ppermute(place[:, :1], "elem", [(i + 1, i) for i in range(count - 1)])
    shape = jax.ShapeDtypeStruct
    kept = pl.pallas_call(
        functools.partial(window_kernel, order),
        out_shape=[
            shape((peers, rows + 2 * slots, segments), f32),
            shape((2 * patches, 2 * slots * peers), bf16),
            shape((nodes, 2 * segments), bf16),
            shape((nodes, 2 * segments), bf16),
            shape((3, patches, nodes), f32),
            shape((patches, nodes), f32),
        ],
        in_specs=[VMEM] * 11,
        out_specs=[VMEM] * 6,
        compiler_params=SMALL,
        cost_estimate=pl.CostEstimate(flops=6 * 3 * patches * nodes * nodes, bytes_accessed=4 * peers * rows * segments, transcendentals=0),
    )(sent, send, pair_slave, place, speed, before, after, inv_mass, stiffness, slave_shape, master_shape)
    velocity, contact = pl.pallas_call(
        force_kernel,
        out_shape=[shape((3, patches, nodes), f32)] * 2,
        in_specs=[VMEM] * 7,
        out_specs=[VMEM] * 2,
        scratch_shapes=[pltpu.VMEM((2 * slots * peers, 3 * segments), bf16)] * 2,
        compiler_params=SMALL,
    )(got, *kept)
    return jnp.transpose(velocity, (1, 0, 2)), jnp.transpose(contact, (1, 0, 2))


def solution(mesh):
    both = ("dom", "elem")
    placed = (
        P(both, None, None),
        P(both, None, None),
        P(both, None),
        P(both, None, None),
        P(both, None),
        P(both, None),
        P(both, None, None),
        P(both, None, None, None),
        P(),
        P(),
        P(),
    )
    return jax.shard_map(
        on_device,
        mesh=mesh,
        in_specs=placed,
        out_specs=(P(both, None, None), P(both, None, None)),
        check_vma=False,
    )
```

time: 30.2 us -> 27.2 us (0.901)
  the two profiles are of different devices: /device:TPU:0 before, /device:TPU:1 now
where the time goes in v2:
time: 27.2 us; the launch traced here: 26.9 us
  starting transfers between devices  12.7 us (47%)
  waiting for transfers between devices  9.32 us (34%)
  Pallas kernels  4.07 us (15%)
  between operations  0.8 us (3%)
    all_to_all x1, waiting for transfers between devices, on_device(): lax.all_to_all(sent, EXCHANGE, split_axis=0, concat_axis=0, tiled=True)  8.62 us
    all_to_all x1, starting transfers between devices, on_device(): lax.all_to_all(sent, EXCHANGE, split_axis=0, concat_axis=0, tiled=True)  7.09 us
    ppermute x1, starting transfers between devices, on_device(): lax.ppermute(place[:, -1:], 'elem', [(i, i + 1) for i in range(count - 1)])  3.4 us
    pallas_call x1, Pallas kernels, on_device(): pl.pallas_call(functools.partial(pack_kernel, order), out_shape=jax.Shape...  2.51 us
    ppermute x1, starting transfers between devices, on_device(): lax.ppermute(place[:, :1], 'elem', [(i + 1, i) for i in range(count - 1)])  2.17 us
    pallas_call x1, Pallas kernels, on_device(): pl.pallas_call(force_kernel, out_shape=[shape((3, patches, nodes), f32)]...  1.32 us
    ppermute x1, waiting for transfers between devices, on_device(): lax.ppermute(place[:, -1:], 'elem', [(i, i + 1) for i in range(count - 1)])  0.7 us
  transfers between devices with their start and end apart: 3, of which 2 were waited for; matrix products, arithmetic and copies ran while one was open for 0% of the time, Pallas kernels for 1%

profile of v2, /device:TPU:1, one launch (start us, length us, event | category | flops | bytes accessed | tf_op | source)
XLA Modules:
  0.0 26.9 jit_solution(6164858306541892771)
XLA Ops:
  0.6 2.5 %shard_map.122.sent_ref = f32[32,32,128]{2,1,0:T(8,128)} custom-call(s32[4,32]{1,0:T(4,128)} %bitcast.16, s32[1,128]{1,0:T(1,128)} %slave_ref.1, f32[3,64,128]{2,1,0:T(8,128)} %bitcast.11, f32[3,64,128]{2,1,0:T(8,128)} %bitcast.14, f32[128,128]{1,0:T(8,128)} %master_shape_ref.1, f32[128,128]{1,0:T(8,128)} %slave_shape_ref.1, f32[3,128,128]{2,1,0:T(8,128)} %bitcast.18, ...), custom_call_target="tpu_custom_call" | custom-call | tf_op jit(solution)/shard_map/pallas_call | solution.py:210
  3.1 0.0 copy-start.1
  3.2 0.0 copy-start
  3.2 0.0 copy-start.2
  3.2 0.0 copy-start.3
  3.2 0.0 copy-start.4
  3.2 0.0 copy-start.5
  3.2 0.0 copy-start.6
  3.2 7.1 %all-to-all-start = ((f32[32,32,128]{2,1,0:T(8,128)}), f32[32,32,128]{2,1,0:T(8,128)S(1)}, u32[]{:S(2)}, u32[]{:S(2)}) async-start(f32[32,32,128]{2,1,0:T(8,128)} %shard_map.122.sent_ref), calls=%async_computation | async-start | bytes 1048576 | tf_op jit(solution)/shard_map/all_to_all | solution.py:218
  10.3 0.0 copy-done.1
  10.3 0.0 copy-start.7
  10.4 0.0 copy-start.8
  10.4 2.2 %collective-permute-start.1 = (f32[3,1,128]{2,1,0:T(1,128)S(1)}, f32[3,1,128]{2,1,0:T(1,128)S(1)}, u32[]{:S(2)}, u32[]{:S(2)}) collective-permute-start(f32[3,1,128]{2,1,0:T(1,128)S(1)} %get-tuple-element.18), channel_id=1, source_target_pairs={{1,0},{2,1},{3,2},{4,3},{5,4},{6,5},{7,6},{9,8},{10,9},{11,10},{12... | collective-permute-start | bytes 4616 | tf_op jit(solution)/shard_map/ppermute | solution.py:221
  12.5 3.4 %collective-permute-start = (f32[3,1,128]{2,1,0:T(1,128)S(1)}, f32[3,1,128]{2,1,0:T(1,128)S(1)}, u32[]{:S(2)}, u32[]{:S(2)}) collective-permute-start(f32[3,1,128]{2,1,0:T(1,128)S(1)} %get-tuple-element.19), channel_id=1, source_target_pairs={{0,1},{1,2},{2,3},{3,4},{4,5},{5,6},{6,7},{8,9},{9,10},{10,11},{11... | collective-permute-start | bytes 4616 | tf_op jit(solution)/shard_map/ppermute | solution.py:220
  16.0 0.0 collective-permute-done.1.after_ref
  16.0 0.7 %collective-permute-done.before_ref = f32[3,1,128]{2,1,0:T(1,128)S(1)} collective-permute-done((f32[3,1,128]{2,1,0:T(1,128)S(1)}, f32[3,1,128]{2,1,0:T(1,128)S(1)}, u32[]{:S(2)}, u32[]{:S(2)}) %collective-permute-start) | collective-permute-done | bytes 1568 | tf_op jit(solution)/shard_map/ppermute | solution.py:220
  16.7 0.0 copy-done
  16.7 0.0 copy-done.2
  16.7 0.0 copy-done.3
  16.7 0.0 copy-done.4
  16.7 0.0 copy-done.5
  16.7 0.0 copy-done.6
  16.7 0.0 copy-done.7
  16.7 0.0 copy-done.8
  16.7 0.2 shard_map.123
  17.0 8.6 %all-to-all-done.got_ref = f32[32,32,128]{2,1,0:T(8,128)S(1)} async-done(((f32[32,32,128]{2,1,0:T(8,128)}), f32[32,32,128]{2,1,0:T(8,128)S(1)}, u32[]{:S(2)}, u32[]{:S(2)}) %all-to-all-start) | async-done | bytes 524320 | tf_op jit(solution)/shard_map/all_to_all | solution.py:218
  25.6 1.3 %shard_map.124 = (f32[3,64,128]{2,1,0:T(8,128)}, f32[3,64,128]{2,1,0:T(8,128)}) custom-call(f32[32,32,128]{2,1,0:T(8,128)S(1)} %all-to-all-done.got_ref, f32[32,40,128]{2,1,0:T(8,128)S(1)} %get-tuple-element.10.own_ref, bf16[128,256]{1,0:T(8,128)(2,1)S(1)} %get-tuple-element.11.table_ref, bf16[128,256]{1,0:T(8,128)(2,1)S(1)} %get-tuple-element.12.shape_high_ref, ...), custom_call_target="tpu_custom_call" | custom-call | tf_op jit(solution)/shard_map/pallas_call | solution.py:238
  (1 shorter events, 0.0 us)
Async XLA Ops:
  3.1 7.2 %copy-start.1 = (f32[64,3,128]{2,0,1:T(8,128)S(1)}, f32[64,3,128]{2,0,1:T(8,128)}, u32[]{:S(2)}) copy-start(f32[64,3,128]{2,0,1:T(8,128)} %param.11) | copy-start | bytes 294916
  3.2 13.5 %copy-start = (f32[32,32,128]{2,1,0:T(8,128)S(1)}, f32[32,32,128]{2,1,0:T(8,128)}, u32[]{:S(2)}) copy-start(f32[32,32,128]{2,1,0:T(8,128)} %shard_map.122.sent_ref) | copy-start | bytes 1572868
  3.2 13.5 %copy-start.2 = (f32[64,3,128]{2,0,1:T(8,128)S(1)}, f32[64,3,128]{2,0,1:T(8,128)}, u32[]{:S(2)}) copy-start(f32[64,3,128]{2,0,1:T(8,128)} %param.12) | copy-start | bytes 294916
  3.2 13.5 %copy-start.3 = (f32[128,128]{1,0:T(8,128)S(1)}, f32[128,128]{1,0:T(8,128)}, u32[]{:S(2)}) copy-start(f32[128,128]{1,0:T(8,128)} %master_shape_ref.1) | copy-start | bytes 196612
  3.2 13.5 %copy-start.4 = (f32[128,128]{1,0:T(8,128)S(1)}, f32[128,128]{1,0:T(8,128)}, u32[]{:S(2)}) copy-start(f32[128,128]{1,0:T(8,128)} %slave_shape_ref.1) | copy-start | bytes 196612
  3.2 13.5 %copy-start.5 = (f32[128,128]{1,0:T(8,128)S(1)}, f32[128,128]{1,0:T(8,128)}, u32[]{:S(2)}) copy-start(f32[128,128]{1,0:T(8,128)} %stiffness_ref.1) | copy-start | bytes 196612
  3.2 13.5 %copy-start.6 = (f32[64,128]{1,0:T(8,128)S(1)}, f32[64,128]{1,0:T(8,128)}, u32[]{:S(2)}) copy-start(f32[64,128]{1,0:T(8,128)} %mass_ref.1) | copy-start | bytes 98308
  3.2 22.4 %all-to-all-start = ((f32[32,32,128]{2,1,0:T(8,128)}), f32[32,32,128]{2,1,0:T(8,128)S(1)}, u32[]{:S(2)}, u32[]{:S(2)}) async-start(f32[32,32,128]{2,1,0:T(8,128)} %shard_map.122.sent_ref), calls=%async_computation | async-start | bytes 1048576 | tf_op jit(solution)/shard_map/all_to_all | solution.py:218
  10.3 6.3 %copy-start.7 = (s32[1,32,4]{1,2,0:T(4,128)S(1)}, s32[1,32,4]{1,2,0:T(4,128)}, u32[]{:S(2)}) copy-start(s32[1,32,4]{1,2,0:T(4,128)} %param.14) | copy-start | bytes 1540
  10.4 6.3 %copy-start.8 = (s32[1,128]{1,0:T(1,128)S(1)}, s32[1,128]{1,0:T(1,128)}, u32[]{:S(2)}) copy-start(s32[1,128]{1,0:T(1,128)} %slave_ref.1) | copy-start | bytes 1540
  10.4 5.6 %collective-permute-start.1 = (f32[3,1,128]{2,1,0:T(1,128)S(1)}, f32[3,1,128]{2,1,0:T(1,128)S(1)}, u32[]{:S(2)}, u32[]{:S(2)}) collective-permute-start(f32[3,1,128]{2,1,0:T(1,128)S(1)} %get-tuple-element.18), channel_id=1, source_target_pairs={{1,0},{2,1},{3,2},{4,3},{5,4},{6,5},{7,6},{9,8},{10,9},{11,10},{12... | collective-permute-start | bytes 4616 | tf_op jit(solution)/shard_map/ppermute | solution.py:221
  12.5 4.1 %collective-permute-start = (f32[3,1,128]{2,1,0:T(1,128)S(1)}, f32[3,1,128]{2,1,0:T(1,128)S(1)}, u32[]{:S(2)}, u32[]{:S(2)}) collective-permute-start(f32[3,1,128]{2,1,0:T(1,128)S(1)} %get-tuple-element.19), channel_id=1, source_target_pairs={{0,1},{1,2},{2,3},{3,4},{4,5},{5,6},{6,7},{8,9},{9,10},{10,11},{11... | collective-permute-start | bytes 4616 | tf_op jit(solution)/shard_map/ppermute | solution.py:220

commit v3 on v2

v3 whole, which is shorter than its diff:
```python
import functools

import jax
import jax.numpy as jnp
from jax import lax
from jax.experimental import pallas as pl
from jax.experimental.pallas import tpu as pltpu
from jax.sharding import PartitionSpec as P

VMEM = pl.BlockSpec(memory_space=pltpu.VMEM)
HBM = pl.BlockSpec(memory_space=pltpu.HBM)
SMALL = pltpu.CompilerParams(vmem_limit_bytes=16 << 20)
BOTH = ("dom", "elem")
NN = (((1,), (0,)), ((), ()))
NT = (((1,), (1,)), ((), ()))
TN = (((0,), (0,)), ((), ()))


def dot(a, b, dims):
    return lax.dot_general(a, b, dims, preferred_element_type=jnp.float32)


def split(x):
    high = x.astype(jnp.bfloat16)
    return high, (x - high.astype(jnp.float32)).astype(jnp.bfloat16)


def dot3(a, b, dims):
    a_high, a_low = split(a)
    b_high, b_low = split(b)
    return dot(a_high, b_high, dims) + (dot(a_high, b_low, dims) + dot(a_low, b_high, dims))


def spot_in_exchange(peer):
    doms, elems = lax.axis_size("dom"), lax.axis_size("elem")
    if doms % 2 or elems % 2:
        return peer
    half = doms // 2
    dom, elem = peer // elems, peer % elems
    return (((elem // 2) * half + dom % half) * 2 + elem % 2) * 2 + (1 - dom // half)


def exchange_order():
    return sorted(range(lax.axis_size("dom") * lax.axis_size("elem")), key=spot_in_exchange)


def index_table(send, slave, patches, master_first):
    slots, peers = send.shape
    width = 2 * slots
    columns = peers * width
    pairs = peers * slots
    master_at, slave_at = (0, slots) if master_first else (slots, 0)

    def iota(shape, dim):
        return lax.broadcasted_iota(jnp.int32, shape, dim)

    column = iota((1, columns), 1)
    spot, place = column // width, column % width
    spread = (spot_in_exchange(iota((peers, 1), 0)) == spot).astype(jnp.bfloat16)
    masters = dot(send.astype(jnp.bfloat16), spread, NN)
    masters = jnp.sum(jnp.where(iota((slots, 1), 0) + master_at == place, masters, 0.0), axis=0, keepdims=True)
    pair = iota((pairs, 1), 0)
    spread = (spot_in_exchange(pair // slots) * width + slave_at + pair % slots == column).astype(jnp.bfloat16)
    slaves = dot((slave + patches).astype(jnp.bfloat16), spread, NN)
    row = (masters + slaves).astype(jnp.int32)
    return (iota((2 * patches, columns), 0) == row).astype(jnp.bfloat16)


def pack_kernel(order, *refs):
    ins, out_hbm, vmem, packed, table_ref, in_sems, out_sems = refs[:9], refs[9], refs[10:19], refs[19], refs[20], refs[21], refs[22]
    loads = [pltpu.make_async_copy(ins[i], vmem[i], in_sems.at[i]) for i in range(9)]
    for load in loads:
        load.start()
    send_ref, slave_ref, live_ref, position_ref, velocity_ref, master_ref, slave_shape_ref, normal_ref, weight_ref = vmem
    _, patches, nodes = position_ref.shape
    slots, peers = send_ref.shape
    segments = weight_ref.shape[-1]
    width = 2 * slots
    for i in (0, 1, 2):
        loads[i].wait()
    table = index_table(send_ref[...], slave_ref[...], patches, True).astype(jnp.float32)
    table = jnp.transpose(table).astype(jnp.bfloat16)
    table_ref[...] = jnp.concatenate([table, table], axis=1)
    live = live_ref[...].astype(jnp.float32).reshape(peers * slots, 1)
    for i in (3, 4, 5, 6):
        loads[i].wait()
    high, low = split((position_ref[...] + 0.5 * velocity_ref[...]).reshape(3 * patches, nodes))
    shape_high, shape_low = split(jnp.concatenate([master_ref[...], slave_shape_ref[...]], axis=1))
    projected = dot(jnp.concatenate([high, low], axis=1), jnp.concatenate([shape_high, shape_high], axis=0), NN)
    projected = (projected + dot(high, shape_low, NN)).reshape(3, patches, 2 * segments)
    loads[7].wait()
    loads[8].wait()
    weight_ref[...] = weight_ref[...] * live
    high, low = split(
        jnp.concatenate([jnp.concatenate([projected[c, :, :segments], projected[c, :, segments:]], axis=0) for c in range(3)], axis=1)
    )
    picked = dot(table_ref[...], jnp.concatenate([high, low], axis=0), NN)
    group = 8
    first = lax.broadcasted_iota(jnp.int32, (group, width, segments), 1) < slots

    def placed(load, peer, half):
        x = load(pl.ds(peer // 2 * width, width))
        x = pltpu.roll(x, slots, 0) if (peer + half) % 2 else x
        return x.reshape(1, width, segments)

    stores = []
    for g in range(0, peers, group):
        gap = jnp.zeros((group, width, segments), jnp.float32)
        for c in range(3):
            chosen = picked[g * width : (g + group) * width, c * segments : (c + 1) * segments].reshape(group, width, segments)
            normal = jnp.concatenate([placed(lambda rows: normal_ref[c, rows, :], p, 1) for p in order[g : g + group]], axis=0)
            gap = gap + normal * chosen
            packed[g : g + group, c * width : (c + 1) * width, :] = jnp.where(first, chosen, normal)
        weight = jnp.concatenate([placed(lambda rows: weight_ref[rows, :], p, 0) for p in order[g : g + group]], axis=0)
        packed[g : g + group, 3 * width : 4 * width, :] = jnp.where(first, weight, gap)
        rows = pl.ds(g, group)
        stores.append(pltpu.make_async_copy(packed.at[rows], out_hbm.at[rows], out_sems.at[g // group]))
        stores[-1].start()
    for store in stores:
        store.wait()


def window_kernel(
    sent_ref, send_ref, slave_ref, position_ref, velocity_ref, before_ref, after_ref, mass_ref, stiffness_ref, slave_shape_ref, master_shape_ref,
    own_ref, table_ref, shape_ref, base_ref, half_ref,
):
    _, patches, nodes = position_ref.shape
    slots, peers = send_ref.shape
    width = 2 * slots
    for t in range(4):
        own_ref[:, t * width : (t + 1) * width, :] = pltpu.roll(sent_ref[:, t * width : (t + 1) * width, :], slots, 1)
    own_ref[:, 4 * width :, :] = sent_ref[:, 3 * width : 4 * width, :]
    table = index_table(send_ref[...], slave_ref[...], patches, False)
    table_ref[...] = jnp.concatenate([table, table], axis=1)
    high, low = split(jnp.concatenate([-master_shape_ref[...], slave_shape_ref[...]], axis=1))
    shape_ref[...] = jnp.concatenate([high, low, high], axis=1)
    row = lax.broadcasted_iota(jnp.int32, (patches, nodes), 0)
    position = position_ref[...]
    product = dot3(position.reshape(3 * patches, nodes), stiffness_ref[...], NN).reshape(3, patches, nodes)
    half = 0.5 * mass_ref[...]
    half_ref[...] = half
    for c in range(3):
        x = position[c]
        before = jnp.where(row == 0, before_ref[c], pltpu.roll(x, 1, 0))
        after = jnp.where(row == patches - 1, after_ref[c], pltpu.roll(x, patches - 1, 0))
        internal = 0.5 * (before + after - 2.0 * x) - product[c]
        base_ref[c] = velocity_ref[c] + half * internal


def force_kernel(got_ref, own_ref, table_ref, shape_ref, base_ref, half_ref, velocity_ref, contact_ref, traction_ref):
    _, patches, nodes = base_ref.shape
    peers, _, segments = got_ref.shape
    width = got_ref.shape[1] // 4
    slots = width // 2
    entries = peers * width
    group = 8

    def tile(ref, g, t):
        return ref[g : g + group, t * width : (t + 1) * width, :]

    first = lax.broadcasted_iota(jnp.int32, (group, width, segments), 1) < slots
    for g in range(0, peers, group):
        last = tile(got_ref, g, 3)
        gap = jnp.where(first, tile(own_ref, g, 3), last)
        for c in range(3):
            gap = gap - tile(got_ref, g, c) * tile(own_ref, g, c)
        weight = jnp.where(first, tile(own_ref, g, 4), pltpu.roll(last, slots, 1))
        pressure = (jnp.maximum(-gap, 0.0) + jnp.log1p(jnp.exp(-jnp.abs(gap)))) * weight
        for c in range(3):
            normal = jnp.where(first, tile(own_ref, g, c), tile(got_ref, g, c))
            high, low = split((normal * pressure).reshape(group * width, segments))
            for at, part in ((0, high), (entries, low)):
                traction_ref[at + g * width : at + (g + group) * width, c * segments : (c + 1) * segments] = part
    summed = dot(table_ref[...], traction_ref[...], NN)
    summed = jnp.concatenate(
        [
            jnp.concatenate([summed[:patches, c * segments : (c + 1) * segments], summed[patches:, c * segments : (c + 1) * segments]], axis=1)
            for c in range(3)
        ],
        axis=0,
    )
    high, low = split(summed)
    contact = dot(jnp.concatenate([high, high, low], axis=1), shape_ref[...], NT).reshape(3, patches, nodes)
    contact_ref[...] = contact
    velocity_ref[...] = base_ref[...] + half_ref[...] * contact


def on_device(
    positions,
    velocities,
    inv_mass,
    send_index,
    pair_slave,
    pair_live,
    quad_weights,
    seg_normals,
    slave_shape,
    master_shape,
    stiffness,
):
    patches, _, nodes = positions.shape
    _, peers, slots = send_index.shape
    segments = quad_weights.shape[-1]
    rows = 8 * slots
    f32, bf16 = jnp.float32, jnp.bfloat16
    order = exchange_order()
    place = jnp.transpose(positions, (1, 0, 2))
    speed = jnp.transpose(velocities, (1, 0, 2))
    send = jnp.transpose(send_index[0], (1, 0))
    normals = jnp.transpose(seg_normals[0], (1, 0, 2))
    operands = (send, pair_slave, pair_live, place, speed, master_shape, slave_shape, normals, quad_weights[0])
    sent = pl.pallas_call(
        functools.partial(pack_kernel, order),
        out_shape=jax.ShapeDtypeStruct((peers, rows, segments), f32),
        in_specs=[HBM] * 9,
        out_specs=HBM,
        scratch_shapes=[pltpu.VMEM(x.shape, x.dtype) for x in operands]
        + [
            pltpu.VMEM((peers, rows, segments), f32),
            pltpu.VMEM((2 * slots * peers, 4 * patches), bf16),
            pltpu.SemaphoreType.DMA((9,)),
            pltpu.SemaphoreType.DMA((peers // 8,)),
        ],
    )(*operands)
    got = lax.all_to_all(sent, BOTH, split_axis=0, concat_axis=0, tiled=True, axis_index_groups=[order])
    count = lax.axis_size("elem")
    before = lax.ppermute(place[:, -1:], "elem", [(i, i + 1) for i in range(count - 1)])
    after = lax.ppermute(place[:, :1], "elem", [(i + 1, i) for i in range(count - 1)])
    shape = jax.ShapeDtypeStruct
    kept = pl.pallas_call(
        window_kernel,
        out_shape=[
            shape((peers, rows + 2 * slots, segments), f32),
            shape((2 * patches, 4 * slots * peers), bf16),
            shape((nodes, 6 * segments), bf16),
            shape((3, patches, nodes), f32),
            shape((patches, nodes), f32),
        ],
        in_specs=[VMEM] * 11,
        out_specs=[VMEM] * 5,
        compiler_params=SMALL,
        cost_estimate=pl.CostEstimate(flops=6 * 3 * patches * nodes * nodes, bytes_accessed=4 * peers * rows * segments, transcendentals=0),
    )(sent, send, pair_slave, place, speed, before, after, inv_mass, stiffness, slave_shape, master_shape)
    velocity, contact = pl.pallas_call(
        force_kernel,
        out_shape=[shape((3, patches, nodes), f32)] * 2,
        in_specs=[VMEM] * 6,
        out_specs=[VMEM] * 2,
        scratch_shapes=[pltpu.VMEM((4 * slots * peers, 3 * segments), bf16)],
        compiler_params=SMALL,
    )(got, *kept)
    return jnp.transpose(velocity, (1, 0, 2)), jnp.transpose(contact, (1, 0, 2))


def solution(mesh):
    both = ("dom", "elem")
    placed = (
        P(both, None, None),
        P(both, None, None),
        P(both, None),
        P(both, None, None),
        P(both, None),
        P(both, None),
        P(both, None, None),
        P(both, None, None, None),
        P(),
        P(),
        P(),
    )
    return jax.shard_map(
        on_device,
        mesh=mesh,
        in_specs=placed,
        out_specs=(P(both, None, None), P(both, None, None)),
        check_vma=False,
    )
```

time: 27.2 us -> 26.5 us (0.974)
  the two profiles are of different devices: /device:TPU:1 before, /device:TPU:0 now
where the time goes in v3:
time: 26.5 us; the launch traced here: 26.2 us
  starting transfers between devices  11.7 us (44%)
  waiting for transfers between devices  9.68 us (37%)
  Pallas kernels  3.97 us (15%)
  between operations  0.8 us (3%)
    all_to_all x1, waiting for transfers between devices, on_device(): lax.all_to_all(sent, BOTH, split_axis=0, concat_axis=0, tiled=True, axis_...  8.88 us
    all_to_all x1, starting transfers between devices, on_device(): lax.all_to_all(sent, BOTH, split_axis=0, concat_axis=0, tiled=True, axis_...  7.33 us
    ppermute x1, starting transfers between devices, on_device(): lax.ppermute(place[:, -1:], 'elem', [(i, i + 1) for i in range(count - 1)])  3.03 us
    pallas_call x1, Pallas kernels, on_device(): pl.pallas_call(functools.partial(pack_kernel, order), out_shape=jax.Shape...  2.38 us
    ppermute x1, starting transfers between devices, on_device(): lax.ppermute(place[:, :1], 'elem', [(i + 1, i) for i in range(count - 1)])  1.29 us
    pallas_call x1, Pallas kernels, on_device(): pl.pallas_call(force_kernel, out_shape=[shape((3, patches, nodes), f32)]...  1.28 us
    ppermute x1, waiting for transfers between devices, on_device(): lax.ppermute(place[:, -1:], 'elem', [(i, i + 1) for i in range(count - 1)])  0.79 us
  transfers between devices with their start and end apart: 3, of which 2 were waited for; matrix products, arithmetic and copies ran while one was open for 0% of the time, Pallas kernels for 1%

profile of v3, /device:TPU:0, one launch (start us, length us, event | category | flops | bytes accessed | tf_op | source)
XLA Modules:
  0.0 26.2 jit_solution(10102805272222403558)
XLA Ops:
  0.6 2.4 %shard_map.122.sent_ref = f32[32,32,128]{2,1,0:T(8,128)} custom-call(s32[4,32]{1,0:T(4,128)} %bitcast.16, s32[1,128]{1,0:T(1,128)} %slave_ref.1, s32[1,128]{1,0:T(1,128)} %refs_2_.1, f32[3,64,128]{2,1,0:T(8,128)} %bitcast.11, f32[3,64,128]{2,1,0:T(8,128)} %bitcast.14, f32[128,128]{1,0:T(8,128)} %master_shape_ref.1, f32[128,128]{1,0:T(8,128)} %slave_shape_ref.1, ...), custom_call_target="tpu_custom_call" | custom-call | tf_op jit(solution)/shard_map/pallas_call | solution.py:212
  3.0 0.0 copy-start.1
  3.0 0.0 copy-start
  3.0 0.0 copy-start.2
  3.0 0.0 copy-start.3
  3.1 0.0 copy-start.4
  3.1 0.0 copy-start.5
  3.1 0.0 copy-start.6
  3.1 7.3 %all-to-all-start = ((f32[32,32,128]{2,1,0:T(8,128)}), f32[32,32,128]{2,1,0:T(8,128)S(1)}, u32[]{:S(2)}, u32[]{:S(2)}) async-start(f32[32,32,128]{2,1,0:T(8,128)} %shard_map.122.sent_ref), calls=%async_computation | async-start | bytes 1048576 | tf_op jit(solution)/shard_map/all_to_all | solution.py:225
  10.4 0.0 copy-done.1
  10.5 0.0 copy-start.7
  10.5 0.0 copy-start.8
  10.5 1.3 %collective-permute-start.1 = (f32[3,1,128]{2,1,0:T(1,128)S(1)}, f32[3,1,128]{2,1,0:T(1,128)S(1)}, u32[]{:S(2)}, u32[]{:S(2)}) collective-permute-start(f32[3,1,128]{2,1,0:T(1,128)S(1)} %get-tuple-element.16), channel_id=1, source_target_pairs={{1,0},{2,1},{3,2},{4,3},{5,4},{6,5},{7,6},{9,8},{10,9},{11,10},{12... | collective-permute-start | bytes 4616 | tf_op jit(solution)/shard_map/ppermute | solution.py:228
  11.8 3.0 %collective-permute-start = (f32[3,1,128]{2,1,0:T(1,128)S(1)}, f32[3,1,128]{2,1,0:T(1,128)S(1)}, u32[]{:S(2)}, u32[]{:S(2)}) collective-permute-start(f32[3,1,128]{2,1,0:T(1,128)S(1)} %get-tuple-element.17), channel_id=1, source_target_pairs={{0,1},{1,2},{2,3},{3,4},{4,5},{5,6},{6,7},{8,9},{9,10},{10,11},{11... | collective-permute-start | bytes 4616 | tf_op jit(solution)/shard_map/ppermute | solution.py:227
  14.8 0.0 collective-permute-done.1.after_ref
  14.8 0.8 %collective-permute-done.before_ref = f32[3,1,128]{2,1,0:T(1,128)S(1)} collective-permute-done((f32[3,1,128]{2,1,0:T(1,128)S(1)}, f32[3,1,128]{2,1,0:T(1,128)S(1)}, u32[]{:S(2)}, u32[]{:S(2)}) %collective-permute-start) | collective-permute-done | bytes 1568 | tf_op jit(solution)/shard_map/ppermute | solution.py:227
  15.6 0.0 copy-done
  15.6 0.0 copy-done.2
  15.6 0.0 copy-done.3
  15.6 0.0 copy-done.4
  15.6 0.0 copy-done.5
  15.6 0.0 copy-done.6
  15.7 0.0 copy-done.7
  15.7 0.0 copy-done.8
  15.7 0.3 %shard_map.123 = (f32[32,40,128]{2,1,0:T(8,128)S(1)}, bf16[128,512]{1,0:T(8,128)(2,1)S(1)}, bf16[128,768]{1,0:T(8,128)(2,1)S(1)}, f32[3,64,128]{2,1,0:T(8,128)S(1)}, f32[64,128]{1,0:T(8,128)S(1)}) custom-call(f32[32,32,128]{2,1,0:T(8,128)S(1)} %copy-done, s32[4,32]{1,0:T(4,128)S(1)} %bitcast.17, s32[1,128]{1,0:T(1,128)S(1)} %copy-done.8, ...), custom_call_target="tpu_custom_call" | custom-call | flops 18874368 | bytes 524288 | tf_op jit(solution)/shard_map/pallas_call | solution.py:230
  16.0 8.9 %all-to-all-done.got_ref = f32[32,32,128]{2,1,0:T(8,128)S(1)} async-done(((f32[32,32,128]{2,1,0:T(8,128)}), f32[32,32,128]{2,1,0:T(8,128)S(1)}, u32[]{:S(2)}, u32[]{:S(2)}) %all-to-all-start) | async-done | bytes 524320 | tf_op jit(solution)/shard_map/all_to_all | solution.py:225
  24.9 1.3 %shard_map.124 = (f32[3,64,128]{2,1,0:T(8,128)}, f32[3,64,128]{2,1,0:T(8,128)}) custom-call(f32[32,32,128]{2,1,0:T(8,128)S(1)} %all-to-all-done.got_ref, f32[32,40,128]{2,1,0:T(8,128)S(1)} %get-tuple-element.9.own_ref, bf16[128,512]{1,0:T(8,128)(2,1)S(1)} %get-tuple-element.10.table_ref, bf16[128,768]{1,0:T(8,128)(2,1)S(1)} %get-tuple-element.11.shape_ref, ...), custom_call_target="tpu_custom_call" | custom-call | tf_op jit(solution)/shard_map/pallas_call | solution.py:244
  (1 shorter events, 0.0 us)
Async XLA Ops:
  3.0 7.4 %copy-start.1 = (f32[64,3,128]{2,0,1:T(8,128)S(1)}, f32[64,3,128]{2,0,1:T(8,128)}, u32[]{:S(2)}) copy-start(f32[64,3,128]{2,0,1:T(8,128)} %param.11) | copy-start | bytes 294916
  3.0 12.6 %copy-start = (f32[32,32,128]{2,1,0:T(8,128)S(1)}, f32[32,32,128]{2,1,0:T(8,128)}, u32[]{:S(2)}) copy-start(f32[32,32,128]{2,1,0:T(8,128)} %shard_map.122.sent_ref) | copy-start | bytes 1572868
  3.0 12.6 %copy-start.2 = (f32[64,3,128]{2,0,1:T(8,128)S(1)}, f32[64,3,128]{2,0,1:T(8,128)}, u32[]{:S(2)}) copy-start(f32[64,3,128]{2,0,1:T(8,128)} %param.12) | copy-start | bytes 294916
  3.0 12.6 %copy-start.3 = (f32[128,128]{1,0:T(8,128)S(1)}, f32[128,128]{1,0:T(8,128)}, u32[]{:S(2)}) copy-start(f32[128,128]{1,0:T(8,128)} %master_shape_ref.1) | copy-start | bytes 196612
  3.1 12.6 %copy-start.4 = (f32[128,128]{1,0:T(8,128)S(1)}, f32[128,128]{1,0:T(8,128)}, u32[]{:S(2)}) copy-start(f32[128,128]{1,0:T(8,128)} %slave_shape_ref.1) | copy-start | bytes 196612
  3.1 12.6 %copy-start.5 = (f32[128,128]{1,0:T(8,128)S(1)}, f32[128,128]{1,0:T(8,128)}, u32[]{:S(2)}) copy-start(f32[128,128]{1,0:T(8,128)} %stiffness_ref.1) | copy-start | bytes 196612
  3.1 12.6 %copy-start.6 = (f32[64,128]{1,0:T(8,128)S(1)}, f32[64,128]{1,0:T(8,128)}, u32[]{:S(2)}) copy-start(f32[64,128]{1,0:T(8,128)} %mass_ref.1) | copy-start | bytes 98308
  3.1 21.8 %all-to-all-start = ((f32[32,32,128]{2,1,0:T(8,128)}), f32[32,32,128]{2,1,0:T(8,128)S(1)}, u32[]{:S(2)}, u32[]{:S(2)}) async-start(f32[32,32,128]{2,1,0:T(8,128)} %shard_map.122.sent_ref), calls=%async_computation | async-start | bytes 1048576 | tf_op jit(solution)/shard_map/all_to_all | solution.py:225
  10.5 5.2 %copy-start.7 = (s32[1,32,4]{1,2,0:T(4,128)S(1)}, s32[1,32,4]{1,2,0:T(4,128)}, u32[]{:S(2)}) copy-start(s32[1,32,4]{1,2,0:T(4,128)} %param.14) | copy-start | bytes 1540
  10.5 5.2 %copy-start.8 = (s32[1,128]{1,0:T(1,128)S(1)}, s32[1,128]{1,0:T(1,128)}, u32[]{:S(2)}) copy-start(s32[1,128]{1,0:T(1,128)} %slave_ref.1) | copy-start | bytes 1540
  10.5 4.3 %collective-permute-start.1 = (f32[3,1,128]{2,1,0:T(1,128)S(1)}, f32[3,1,128]{2,1,0:T(1,128)S(1)}, u32[]{:S(2)}, u32[]{:S(2)}) collective-permute-start(f32[3,1,128]{2,1,0:T(1,128)S(1)} %get-tuple-element.16), channel_id=1, source_target_pairs={{1,0},{2,1},{3,2},{4,3},{5,4},{6,5},{7,6},{9,8},{10,9},{11,10},{12... | collective-permute-start | bytes 4616 | tf_op jit(solution)/shard_map/ppermute | solution.py:228
  11.8 3.8 %collective-permute-start = (f32[3,1,128]{2,1,0:T(1,128)S(1)}, f32[3,1,128]{2,1,0:T(1,128)S(1)}, u32[]{:S(2)}, u32[]{:S(2)}) collective-permute-start(f32[3,1,128]{2,1,0:T(1,128)S(1)} %get-tuple-element.17), channel_id=1, source_target_pairs={{0,1},{1,2},{2,3},{3,4},{4,5},{5,6},{6,7},{8,9},{9,10},{10,11},{11... | collective-permute-start | bytes 4616 | tf_op jit(solution)/shard_map/ppermute | solution.py:227

commit v4 on v3

--- a/solution.py
+++ b/solution.py
@@ -35,6 +35,8 @@
     doms, elems = lax.axis_size("dom"), lax.axis_size("elem")
     if doms % 2 or elems % 2:
         return peer
+    last = doms * elems - 1
+    peer = peer + (peer == 1) * (last - 1) - (peer == last) * (last - 1)
     half = doms // 2
     dom, elem = peer // elems, peer % elems
     return (((elem // 2) * half + dom % half) * 2 + elem % 2) * 2 + (1 - dom // half)

time: 26.5 us -> 26.2 us (0.989)
  waiting for transfers between devices: 9.68 us -> 9.38 us
    all_to_all x1, waiting for transfers between devices: 8.88 us -> 8.59 us  [on_device(): lax.all_to_all(sent, BOTH, split_axis=0, concat_axis=0, tiled=True, axis_...]
where the time goes in v4:
time: 26.2 us; the launch traced here: 25.9 us
  starting transfers between devices  11.7 us (45%)
  waiting for transfers between devices  9.38 us (36%)
  Pallas kernels  4.02 us (15%)
  between operations  0.8 us (3%)
    all_to_all x1, waiting for transfers between devices, on_device(): lax.all_to_all(sent, BOTH, split_axis=0, concat_axis=0, tiled=True, axis_...  8.59 us
    all_to_all x1, starting transfers between devices, on_device(): lax.all_to_all(sent, BOTH, split_axis=0, concat_axis=0, tiled=True, axis_...  7.33 us
    ppermute x1, starting transfers between devices, on_device(): lax.ppermute(place[:, -1:], 'elem', [(i, i + 1) for i in range(count - 1)])  3.03 us
    pallas_call x1, Pallas kernels, on_device(): pl.pallas_call(functools.partial(pack_kernel, order), out_shape=jax.Shape...  2.4 us
    ppermute x1, starting transfers between devices, on_device(): lax.ppermute(place[:, :1], 'elem', [(i + 1, i) for i in range(count - 1)])  1.29 us
    pallas_call x1, Pallas kernels, on_device(): pl.pallas_call(force_kernel, out_shape=[shape((3, patches, nodes), f32)]...  1.28 us
    ppermute x1, waiting for transfers between devices, on_device(): lax.ppermute(place[:, -1:], 'elem', [(i, i + 1) for i in range(count - 1)])  0.79 us
  transfers between devices with their start and end apart: 3, of which 2 were waited for; matrix products, arithmetic and copies ran while one was open for 0% of the time, Pallas kernels for 1%

profile of v4, /device:TPU:0, one launch (start us, length us, event | category | flops | bytes accessed | tf_op | source)
XLA Modules:
  0.0 25.9 jit_solution(10815877277274320457)
XLA Ops:
  0.6 2.4 %shard_map.122.sent_ref = f32[32,32,128]{2,1,0:T(8,128)} custom-call(s32[4,32]{1,0:T(4,128)} %bitcast.16, s32[1,128]{1,0:T(1,128)} %slave_ref.1, s32[1,128]{1,0:T(1,128)} %refs_2_.1, f32[3,64,128]{2,1,0:T(8,128)} %bitcast.11, f32[3,64,128]{2,1,0:T(8,128)} %bitcast.14, f32[128,128]{1,0:T(8,128)} %master_shape_ref.1, f32[128,128]{1,0:T(8,128)} %slave_shape_ref.1, ...), custom_call_target="tpu_custom_call" | custom-call | tf_op jit(solution)/shard_map/pallas_call | solution.py:214
  3.0 0.0 copy-start.1
  3.1 0.0 copy-start
  3.1 0.0 copy-start.2
  3.1 0.0 copy-start.3
  3.1 0.0 copy-start.4
  3.1 0.0 copy-start.5
  3.1 0.0 copy-start.6
  3.1 7.3 %all-to-all-start = ((f32[32,32,128]{2,1,0:T(8,128)}), f32[32,32,128]{2,1,0:T(8,128)S(1)}, u32[]{:S(2)}, u32[]{:S(2)}) async-start(f32[32,32,128]{2,1,0:T(8,128)} %shard_map.122.sent_ref), calls=%async_computation | async-start | bytes 1048576 | tf_op jit(solution)/shard_map/all_to_all | solution.py:227
  10.5 0.0 copy-done.1
  10.5 0.0 copy-start.7
  10.5 0.0 copy-start.8
  10.5 1.3 %collective-permute-start.1 = (f32[3,1,128]{2,1,0:T(1,128)S(1)}, f32[3,1,128]{2,1,0:T(1,128)S(1)}, u32[]{:S(2)}, u32[]{:S(2)}) collective-permute-start(f32[3,1,128]{2,1,0:T(1,128)S(1)} %get-tuple-element.16), channel_id=1, source_target_pairs={{1,0},{2,1},{3,2},{4,3},{5,4},{6,5},{7,6},{9,8},{10,9},{11,10},{12... | collective-permute-start | bytes 4616 | tf_op jit(solution)/shard_map/ppermute | solution.py:230
  11.8 3.0 %collective-permute-start = (f32[3,1,128]{2,1,0:T(1,128)S(1)}, f32[3,1,128]{2,1,0:T(1,128)S(1)}, u32[]{:S(2)}, u32[]{:S(2)}) collective-permute-start(f32[3,1,128]{2,1,0:T(1,128)S(1)} %get-tuple-element.17), channel_id=1, source_target_pairs={{0,1},{1,2},{2,3},{3,4},{4,5},{5,6},{6,7},{8,9},{9,10},{10,11},{11... | collective-permute-start | bytes 4616 | tf_op jit(solution)/shard_map/ppermute | solution.py:229
  14.8 0.0 collective-permute-done.1.after_ref
  14.9 0.8 %collective-permute-done.before_ref = f32[3,1,128]{2,1,0:T(1,128)S(1)} collective-permute-done((f32[3,1,128]{2,1,0:T(1,128)S(1)}, f32[3,1,128]{2,1,0:T(1,128)S(1)}, u32[]{:S(2)}, u32[]{:S(2)}) %collective-permute-start) | collective-permute-done | bytes 1568 | tf_op jit(solution)/shard_map/ppermute | solution.py:229
  15.7 0.0 copy-done
  15.7 0.0 copy-done.2
  15.7 0.0 copy-done.3
  15.7 0.0 copy-done.4
  15.7 0.0 copy-done.5
  15.7 0.0 copy-done.6
  15.7 0.0 copy-done.7
  15.7 0.0 copy-done.8
  15.7 0.3 %shard_map.123 = (f32[32,40,128]{2,1,0:T(8,128)S(1)}, bf16[128,512]{1,0:T(8,128)(2,1)S(1)}, bf16[128,768]{1,0:T(8,128)(2,1)S(1)}, f32[3,64,128]{2,1,0:T(8,128)S(1)}, f32[64,128]{1,0:T(8,128)S(1)}) custom-call(f32[32,32,128]{2,1,0:T(8,128)S(1)} %copy-done, s32[4,32]{1,0:T(4,128)S(1)} %bitcast.17, s32[1,128]{1,0:T(1,128)S(1)} %copy-done.8, ...), custom_call_target="tpu_custom_call" | custom-call | flops 18874368 | bytes 524288 | tf_op jit(solution)/shard_map/pallas_call | solution.py:232
  16.0 8.6 %all-to-all-done.got_ref = f32[32,32,128]{2,1,0:T(8,128)S(1)} async-done(((f32[32,32,128]{2,1,0:T(8,128)}), f32[32,32,128]{2,1,0:T(8,128)S(1)}, u32[]{:S(2)}, u32[]{:S(2)}) %all-to-all-start) | async-done | bytes 524320 | tf_op jit(solution)/shard_map/all_to_all | solution.py:227
  24.6 1.3 %shard_map.124 = (f32[3,64,128]{2,1,0:T(8,128)}, f32[3,64,128]{2,1,0:T(8,128)}) custom-call(f32[32,32,128]{2,1,0:T(8,128)S(1)} %all-to-all-done.got_ref, f32[32,40,128]{2,1,0:T(8,128)S(1)} %get-tuple-element.9.own_ref, bf16[128,512]{1,0:T(8,128)(2,1)S(1)} %get-tuple-element.10.table_ref, bf16[128,768]{1,0:T(8,128)(2,1)S(1)} %get-tuple-element.11.shape_ref, ...), custom_call_target="tpu_custom_call" | custom-call | tf_op jit(solution)/shard_map/pallas_call | solution.py:246
  (1 shorter events, 0.0 us)
Async XLA Ops:
  3.0 7.4 %copy-start.1 = (f32[64,3,128]{2,0,1:T(8,128)S(1)}, f32[64,3,128]{2,0,1:T(8,128)}, u32[]{:S(2)}) copy-start(f32[64,3,128]{2,0,1:T(8,128)} %param.11) | copy-start | bytes 294916
  3.1 12.6 %copy-start = (f32[32,32,128]{2,1,0:T(8,128)S(1)}, f32[32,32,128]{2,1,0:T(8,128)}, u32[]{:S(2)}) copy-start(f32[32,32,128]{2,1,0:T(8,128)} %shard_map.122.sent_ref) | copy-start | bytes 1572868
  3.1 12.6 %copy-start.2 = (f32[64,3,128]{2,0,1:T(8,128)S(1)}, f32[64,3,128]{2,0,1:T(8,128)}, u32[]{:S(2)}) copy-start(f32[64,3,128]{2,0,1:T(8,128)} %param.12) | copy-start | bytes 294916
  3.1 12.6 %copy-start.3 = (f32[128,128]{1,0:T(8,128)S(1)}, f32[128,128]{1,0:T(8,128)}, u32[]{:S(2)}) copy-start(f32[128,128]{1,0:T(8,128)} %master_shape_ref.1) | copy-start | bytes 196612
  3.1 12.6 %copy-start.4 = (f32[128,128]{1,0:T(8,128)S(1)}, f32[128,128]{1,0:T(8,128)}, u32[]{:S(2)}) copy-start(f32[128,128]{1,0:T(8,128)} %slave_shape_ref.1) | copy-start | bytes 196612
  3.1 12.6 %copy-start.5 = (f32[128,128]{1,0:T(8,128)S(1)}, f32[128,128]{1,0:T(8,128)}, u32[]{:S(2)}) copy-start(f32[128,128]{1,0:T(8,128)} %stiffness_ref.1) | copy-start | bytes 196612
  3.1 12.6 %copy-start.6 = (f32[64,128]{1,0:T(8,128)S(1)}, f32[64,128]{1,0:T(8,128)}, u32[]{:S(2)}) copy-start(f32[64,128]{1,0:T(8,128)} %mass_ref.1) | copy-start | bytes 98308
  3.1 21.5 %all-to-all-start = ((f32[32,32,128]{2,1,0:T(8,128)}), f32[32,32,128]{2,1,0:T(8,128)S(1)}, u32[]{:S(2)}, u32[]{:S(2)}) async-start(f32[32,32,128]{2,1,0:T(8,128)} %shard_map.122.sent_ref), calls=%async_computation | async-start | bytes 1048576 | tf_op jit(solution)/shard_map/all_to_all | solution.py:227
  10.5 5.2 %copy-start.7 = (s32[1,32,4]{1,2,0:T(4,128)S(1)}, s32[1,32,4]{1,2,0:T(4,128)}, u32[]{:S(2)}) copy-start(s32[1,32,4]{1,2,0:T(4,128)} %param.14) | copy-start | bytes 1540
  10.5 5.2 %copy-start.8 = (s32[1,128]{1,0:T(1,128)S(1)}, s32[1,128]{1,0:T(1,128)}, u32[]{:S(2)}) copy-start(s32[1,128]{1,0:T(1,128)} %slave_ref.1) | copy-start | bytes 1540
  10.5 4.3 %collective-permute-start.1 = (f32[3,1,128]{2,1,0:T(1,128)S(1)}, f32[3,1,128]{2,1,0:T(1,128)S(1)}, u32[]{:S(2)}, u32[]{:S(2)}) collective-permute-start(f32[3,1,128]{2,1,0:T(1,128)S(1)} %get-tuple-element.16), channel_id=1, source_target_pairs={{1,0},{2,1},{3,2},{4,3},{5,4},{6,5},{7,6},{9,8},{10,9},{11,10},{12... | collective-permute-start | bytes 4616 | tf_op jit(solution)/shard_map/ppermute | solution.py:230
  11.8 3.8 %collective-permute-start = (f32[3,1,128]{2,1,0:T(1,128)S(1)}, f32[3,1,128]{2,1,0:T(1,128)S(1)}, u32[]{:S(2)}, u32[]{:S(2)}) collective-permute-start(f32[3,1,128]{2,1,0:T(1,128)S(1)} %get-tuple-element.17), channel_id=1, source_target_pairs={{0,1},{1,2},{2,3},{3,4},{4,5},{5,6},{6,7},{8,9},{9,10},{10,11},{11... | collective-permute-start | bytes 4616 | tf_op jit(solution)/shard_map/ppermute | solution.py:229

commit v5 on v4

--- a/solution.py
+++ b/solution.py
@@ -36,7 +36,8 @@
     if doms % 2 or elems % 2:
         return peer
     last = doms * elems - 1
-    peer = peer + (peer == 1) * (last - 1) - (peer == last) * (last - 1)
+    for a, b in ((1, last), (elems, last - 1)):
+        peer = peer + (peer == a) * (b - a) + (peer == b) * (a - b)
     half = doms // 2
     dom, elem = peer // elems, peer % elems
     return (((elem // 2) * half + dom % half) * 2 + elem % 2) * 2 + (1 - dom // half)

time: 26.2 us -> 25.8 us (0.985)
  waiting for transfers between devices: 9.38 us -> 8.91 us
    all_to_all x1, waiting for transfers between devices: 8.59 us -> 8.12 us  [on_device(): lax.all_to_all(sent, BOTH, split_axis=0, concat_axis=0, tiled=True, axis_...]
where the time goes in v5:
time: 25.8 us; the launch traced here: 25.5 us
  starting transfers between devices  11.7 us (45%)
  waiting for transfers between devices  8.91 us (35%)
  Pallas kernels  4.07 us (16%)
  between operations  0.8 us (3%)
    all_to_all x1, waiting for transfers between devices, on_device(): lax.all_to_all(sent, BOTH, split_axis=0, concat_axis=0, tiled=True, axis_...  8.12 us
    all_to_all x1, starting transfers between devices, on_device(): lax.all_to_all(sent, BOTH, split_axis=0, concat_axis=0, tiled=True, axis_...  7.33 us
    ppermute x1, starting transfers between devices, on_device(): lax.ppermute(place[:, -1:], 'elem', [(i, i + 1) for i in range(count - 1)])  3.03 us
    pallas_call x1, Pallas kernels, on_device(): pl.pallas_call(functools.partial(pack_kernel, order), out_shape=jax.Shape...  2.43 us
    ppermute x1, starting transfers between devices, on_device(): lax.ppermute(place[:, :1], 'elem', [(i + 1, i) for i in range(count - 1)])  1.29 us
    pallas_call x1, Pallas kernels, on_device(): pl.pallas_call(force_kernel, out_shape=[shape((3, patches, nodes), f32)]...  1.28 us
    ppermute x1, waiting for transfers between devices, on_device(): lax.ppermute(place[:, -1:], 'elem', [(i, i + 1) for i in range(count - 1)])  0.79 us
  transfers between devices with their start and end apart: 3, of which 2 were waited for; matrix products, arithmetic and copies ran while one was open for 0% of the time, Pallas kernels for 1%

profile of v5, /device:TPU:0, one launch (start us, length us, event | category | flops | bytes accessed | tf_op | source)
XLA Modules:
  0.0 25.5 jit_solution(9695811900688027158)
XLA Ops:
  0.6 2.4 %shard_map.122.sent_ref = f32[32,32,128]{2,1,0:T(8,128)} custom-call(s32[4,32]{1,0:T(4,128)} %bitcast.16, s32[1,128]{1,0:T(1,128)} %slave_ref.1, s32[1,128]{1,0:T(1,128)} %refs_2_.1, f32[3,64,128]{2,1,0:T(8,128)} %bitcast.11, f32[3,64,128]{2,1,0:T(8,128)} %bitcast.14, f32[128,128]{1,0:T(8,128)} %master_shape_ref.1, f32[128,128]{1,0:T(8,128)} %slave_shape_ref.1, ...), custom_call_target="tpu_custom_call" | custom-call | tf_op jit(solution)/shard_map/pallas_call | solution.py:215
  3.1 0.0 copy-start.1
  3.1 0.0 copy-start
  3.1 0.0 copy-start.2
  3.1 0.0 copy-start.3
  3.1 0.0 copy-start.4
  3.1 0.0 copy-start.5
  3.1 0.0 copy-start.6
  3.1 7.3 %all-to-all-start = ((f32[32,32,128]{2,1,0:T(8,128)}), f32[32,32,128]{2,1,0:T(8,128)S(1)}, u32[]{:S(2)}, u32[]{:S(2)}) async-start(f32[32,32,128]{2,1,0:T(8,128)} %shard_map.122.sent_ref), calls=%async_computation | async-start | bytes 1048576 | tf_op jit(solution)/shard_map/all_to_all | solution.py:228
  10.5 0.0 copy-done.1
  10.5 0.0 copy-start.7
  10.5 0.0 copy-start.8
  10.5 1.3 %collective-permute-start.1 = (f32[3,1,128]{2,1,0:T(1,128)S(1)}, f32[3,1,128]{2,1,0:T(1,128)S(1)}, u32[]{:S(2)}, u32[]{:S(2)}) collective-permute-start(f32[3,1,128]{2,1,0:T(1,128)S(1)} %get-tuple-element.16), channel_id=1, source_target_pairs={{1,0},{2,1},{3,2},{4,3},{5,4},{6,5},{7,6},{9,8},{10,9},{11,10},{12... | collective-permute-start | bytes 4616 | tf_op jit(solution)/shard_map/ppermute | solution.py:231
  11.8 3.0 %collective-permute-start = (f32[3,1,128]{2,1,0:T(1,128)S(1)}, f32[3,1,128]{2,1,0:T(1,128)S(1)}, u32[]{:S(2)}, u32[]{:S(2)}) collective-permute-start(f32[3,1,128]{2,1,0:T(1,128)S(1)} %get-tuple-element.17), channel_id=1, source_target_pairs={{0,1},{1,2},{2,3},{3,4},{4,5},{5,6},{6,7},{8,9},{9,10},{10,11},{11... | collective-permute-start | bytes 4616 | tf_op jit(solution)/shard_map/ppermute | solution.py:230
  14.9 0.0 collective-permute-done.1.after_ref
  14.9 0.8 %collective-permute-done.before_ref = f32[3,1,128]{2,1,0:T(1,128)S(1)} collective-permute-done((f32[3,1,128]{2,1,0:T(1,128)S(1)}, f32[3,1,128]{2,1,0:T(1,128)S(1)}, u32[]{:S(2)}, u32[]{:S(2)}) %collective-permute-start) | collective-permute-done | bytes 1568 | tf_op jit(solution)/shard_map/ppermute | solution.py:230
  15.7 0.0 copy-done
  15.7 0.0 copy-done.2
  15.7 0.0 copy-done.3
  15.7 0.0 copy-done.4
  15.7 0.0 copy-done.5
  15.7 0.0 copy-done.6
  15.7 0.0 copy-done.7
  15.7 0.0 copy-done.8
  15.7 0.4 %shard_map.123 = (f32[32,40,128]{2,1,0:T(8,128)S(1)}, bf16[128,512]{1,0:T(8,128)(2,1)S(1)}, bf16[128,768]{1,0:T(8,128)(2,1)S(1)}, f32[3,64,128]{2,1,0:T(8,128)S(1)}, f32[64,128]{1,0:T(8,128)S(1)}) custom-call(f32[32,32,128]{2,1,0:T(8,128)S(1)} %copy-done, s32[4,32]{1,0:T(4,128)S(1)} %bitcast.17, s32[1,128]{1,0:T(1,128)S(1)} %copy-done.8, ...), custom_call_target="tpu_custom_call" | custom-call | flops 18874368 | bytes 524288 | tf_op jit(solution)/shard_map/pallas_call | solution.py:233
  16.1 8.1 %all-to-all-done.got_ref = f32[32,32,128]{2,1,0:T(8,128)S(1)} async-done(((f32[32,32,128]{2,1,0:T(8,128)}), f32[32,32,128]{2,1,0:T(8,128)S(1)}, u32[]{:S(2)}, u32[]{:S(2)}) %all-to-all-start) | async-done | bytes 524320 | tf_op jit(solution)/shard_map/all_to_all | solution.py:228
  24.2 1.3 %shard_map.124 = (f32[3,64,128]{2,1,0:T(8,128)}, f32[3,64,128]{2,1,0:T(8,128)}) custom-call(f32[32,32,128]{2,1,0:T(8,128)S(1)} %all-to-all-done.got_ref, f32[32,40,128]{2,1,0:T(8,128)S(1)} %get-tuple-element.9.own_ref, bf16[128,512]{1,0:T(8,128)(2,1)S(1)} %get-tuple-element.10.table_ref, bf16[128,768]{1,0:T(8,128)(2,1)S(1)} %get-tuple-element.11.shape_ref, ...), custom_call_target="tpu_custom_call" | custom-call | tf_op jit(solution)/shard_map/pallas_call | solution.py:247
  (1 shorter events, 0.0 us)
Async XLA Ops:
  3.1 7.4 %copy-start.1 = (f32[64,3,128]{2,0,1:T(8,128)S(1)}, f32[64,3,128]{2,0,1:T(8,128)}, u32[]{:S(2)}) copy-start(f32[64,3,128]{2,0,1:T(8,128)} %param.11) | copy-start | bytes 294916
  3.1 12.6 %copy-start = (f32[32,32,128]{2,1,0:T(8,128)S(1)}, f32[32,32,128]{2,1,0:T(8,128)}, u32[]{:S(2)}) copy-start(f32[32,32,128]{2,1,0:T(8,128)} %shard_map.122.sent_ref) | copy-start | bytes 1572868
  3.1 12.6 %copy-start.2 = (f32[64,3,128]{2,0,1:T(8,128)S(1)}, f32[64,3,128]{2,0,1:T(8,128)}, u32[]{:S(2)}) copy-start(f32[64,3,128]{2,0,1:T(8,128)} %param.12) | copy-start | bytes 294916
  3.1 12.6 %copy-start.3 = (f32[128,128]{1,0:T(8,128)S(1)}, f32[128,128]{1,0:T(8,128)}, u32[]{:S(2)}) copy-start(f32[128,128]{1,0:T(8,128)} %master_shape_ref.1) | copy-start | bytes 196612
  3.1 12.6 %copy-start.4 = (f32[128,128]{1,0:T(8,128)S(1)}, f32[128,128]{1,0:T(8,128)}, u32[]{:S(2)}) copy-start(f32[128,128]{1,0:T(8,128)} %slave_shape_ref.1) | copy-start | bytes 196612
  3.1 12.6 %copy-start.5 = (f32[128,128]{1,0:T(8,128)S(1)}, f32[128,128]{1,0:T(8,128)}, u32[]{:S(2)}) copy-start(f32[128,128]{1,0:T(8,128)} %stiffness_ref.1) | copy-start | bytes 196612
  3.1 12.6 %copy-start.6 = (f32[64,128]{1,0:T(8,128)S(1)}, f32[64,128]{1,0:T(8,128)}, u32[]{:S(2)}) copy-start(f32[64,128]{1,0:T(8,128)} %mass_ref.1) | copy-start | bytes 98308
  3.1 21.1 %all-to-all-start = ((f32[32,32,128]{2,1,0:T(8,128)}), f32[32,32,128]{2,1,0:T(8,128)S(1)}, u32[]{:S(2)}, u32[]{:S(2)}) async-start(f32[32,32,128]{2,1,0:T(8,128)} %shard_map.122.sent_ref), calls=%async_computation | async-start | bytes 1048576 | tf_op jit(solution)/shard_map/all_to_all | solution.py:228
  10.5 5.2 %copy-start.7 = (s32[1,32,4]{1,2,0:T(4,128)S(1)}, s32[1,32,4]{1,2,0:T(4,128)}, u32[]{:S(2)}) copy-start(s32[1,32,4]{1,2,0:T(4,128)} %param.14) | copy-start | bytes 1540
  10.5 5.2 %copy-start.8 = (s32[1,128]{1,0:T(1,128)S(1)}, s32[1,128]{1,0:T(1,128)}, u32[]{:S(2)}) copy-start(s32[1,128]{1,0:T(1,128)} %slave_ref.1) | copy-start | bytes 1540
  10.5 4.3 %collective-permute-start.1 = (f32[3,1,128]{2,1,0:T(1,128)S(1)}, f32[3,1,128]{2,1,0:T(1,128)S(1)}, u32[]{:S(2)}, u32[]{:S(2)}) collective-permute-start(f32[3,1,128]{2,1,0:T(1,128)S(1)} %get-tuple-element.16), channel_id=1, source_target_pairs={{1,0},{2,1},{3,2},{4,3},{5,4},{6,5},{7,6},{9,8},{10,9},{11,10},{12... | collective-permute-start | bytes 4616 | tf_op jit(solution)/shard_map/ppermute | solution.py:231
  11.8 3.8 %collective-permute-start = (f32[3,1,128]{2,1,0:T(1,128)S(1)}, f32[3,1,128]{2,1,0:T(1,128)S(1)}, u32[]{:S(2)}, u32[]{:S(2)}) collective-permute-start(f32[3,1,128]{2,1,0:T(1,128)S(1)} %get-tuple-element.17), channel_id=1, source_target_pairs={{0,1},{1,2},{2,3},{3,4},{4,5},{5,6},{6,7},{8,9},{9,10},{10,11},{11... | collective-permute-start | bytes 4616 | tf_op jit(solution)/shard_map/ppermute | solution.py:230
